TPU v7x, 32 devices: a whole 2x2x4 slice. The times are simulated.
32 devices in a mesh: wide: 8 (over z, x), narrow: 4 (over y, core).
Axes of the slice: x: 2, y: 2, z: 4, core: 2. Of those that a mesh axis runs over, the one named last changes fastest.
Arguments:
- tokens: bfloat16 [26880, 768], P(('wide', 'narrow')), may hold values from -6 to 6
- patch_counts: int32 [96], P('wide'), may hold values from 100 to 240, as said below
- ln1_gain: float32 [768], replicated, may hold values from 0.25 to 1.75
- ln1_bias: float32 [768], replicated, may hold values from -3 to 3
- w_qkv: bfloat16 [768, 3, 768], P(None, None, 'narrow'), may hold values from -0.21875 to 0.21875
- b_qv: float32 [2, 768], P(None, 'narrow'), may hold values from -3 to 3
- w_out: bfloat16 [768, 768], P('narrow'), may hold values from -0.625 to 0.625
- b_out: float32 [768], replicated, may hold values from -3 to 3
- ln2_gain: float32 [768], replicated, may hold values from 0.25 to 1.75
- ln2_bias: float32 [768], replicated, may hold values from -3 to 3
- w_up: bfloat16 [768, 3072], P(None, 'narrow'), may hold values from -0.21875 to 0.21875
- b_up: bfloat16 [1, 3072], P(None, 'narrow'), may hold values from -3 to 3
- w_down: bfloat16 [3072, 768], P('narrow'), may hold values from -0.109375 to 0.109375
- b_down: float32 [768], replicated, may hold values from -3 to 3
- cotangent: bfloat16 [26880, 768], P(('wide', 'narrow')), may hold values from -6 to 6
Outputs:
- layer_out: float32 [26880, 768], P(('wide', 'narrow'))
- input_grad: float32 [26880, 768], P(('wide', 'narrow'))
- ln1_gain_grad: float32 [768], replicated
- ln1_bias_grad: float32 [768], replicated
- w_qkv_grad: float32 [768, 3, 768], P(None, None, 'narrow')
- b_qv_grad: float32 [2, 768], P(None, 'narrow')
- w_out_grad: float32 [768, 768], P('narrow')
- b_out_grad: float32 [768], replicated
- ln2_gain_grad: float32 [768], replicated
- ln2_bias_grad: float32 [768], replicated
- w_up_grad: float32 [768, 3072], P(None, 'narrow')
- b_up_grad: float32 [1, 3072], P(None, 'narrow')
- w_down_grad: float32 [3072, 768], P('narrow')
- b_down_grad: float32 [768], replicated
Inputs may be any that keep to these rules, and one draw needn't show every extreme that they name: patch_counts[i] is the number of real patches of item i; key positions 40 + patch_counts[i] and later of that item are padding.
All inputs are finite; a program needn't handle non-finite values.
Results may differ from a plain program's by a relative error of at most 0.012.
The roundings to bfloat16 on the way count: a program that leaves them out, or rounds other values in their place, can miss the bound.
Values may be sent and summed in bfloat16 or wider, within the bound.
No kernel may reach another device: no remote copies, remote signals or barrier semaphores. Data moves between devices by JAX's collectives and lax.ppermute only.
A program may use at most 192 MiB of HBM per device.

v0:
```python
import jax
import jax.numpy as jnp
from jax import lax
from jax.sharding import PartitionSpec as P

HEAD = 64
WORDS = 40


norm_eps = 1e-06
masked_value = -1000000000.0


def norm_parts(inputs, gain_row, bias_row):
    mean_rows = jnp.mean(inputs, axis=-1, keepdims=True)
    centred = inputs - mean_rows
    var_rows = jnp.mean(centred * centred, axis=-1, keepdims=True)
    inv_scale = lax.rsqrt(var_rows + norm_eps)
    unit_rows = centred * inv_scale
    return (unit_rows * gain_row + bias_row, unit_rows, inv_scale)


def norm_back(grad_rows, unit_rows, inv_scale, gain_row):
    scaled = grad_rows * gain_row
    inner = (
        scaled
        - jnp.mean(scaled, axis=-1, keepdims=True)
        - unit_rows * jnp.mean(scaled * unit_rows, axis=-1, keepdims=True)
    )
    return (inv_scale * inner, jnp.sum(grad_rows * unit_rows, axis=0), jnp.sum(grad_rows, axis=0))


def contract_rows(left_side, right_side):
    return lax.dot_general(
        left_side, right_side, (((0,), (0,)), ((), ())), preferred_element_type=jnp.float32
    )


def contract_cols(left_side, right_side):
    return lax.dot_general(
        left_side, right_side, (((1,), (1,)), ((), ())), preferred_element_type=jnp.float32
    )


def gelu_exact(inputs):
    return jax.nn.gelu(inputs, approximate=False)


def on_device(
    tokens,
    patch_counts,
    ln1_gain,
    ln1_bias,
    w_qkv,
    b_qv,
    w_out,
    b_out,
    ln2_gain,
    ln2_bias,
    w_up,
    b_up,
    w_down,
    b_down,
    cotangent,
):
    inputs = tokens.astype(jnp.float32)
    normed1, unit1, inv1 = norm_parts(inputs, ln1_gain, ln1_bias)
    normed1 = normed1.astype(jnp.bfloat16)
    grouped = lax.all_gather(normed1, "narrow", axis=0, tiled=True)
    full_out, full_down = (
        lax.all_gather(w_out, "narrow", axis=0, tiled=True),
        lax.all_gather(w_down, "narrow", axis=0, tiled=True),
    )
    full_up, full_up_bias = (
        lax.all_gather(w_up, "narrow", axis=1, tiled=True),
        lax.all_gather(b_up, "narrow", axis=1, tiled=True),
    )
    projected = jnp.einsum("td,dcf->tcf", grouped, w_qkv, preferred_element_type=jnp.float32)
    queries = ((projected[:, 0] + b_qv[0]) * 0.125).astype(jnp.bfloat16)
    key_rows = projected[:, 1].astype(jnp.bfloat16)
    value_rows = (projected[:, 2] + b_qv[1]).astype(jnp.bfloat16)
    item_count = patch_counts.shape[0]
    head_cols = w_qkv.shape[2]
    group_rows = grouped.shape[0]
    seq_len = group_rows // item_count
    shaped = (item_count, seq_len, head_cols // HEAD, HEAD)
    query_four = queries.reshape(shaped)
    key_four = key_rows.reshape(shaped)
    value_four = value_rows.reshape(shaped)
    positions = jnp.arange(seq_len)
    valid_keys = positions[None, :] < (WORDS + patch_counts)[:, None]
    key_mask = jnp.where(valid_keys, 0.0, masked_value).astype(jnp.float32)[:, None, None, :]
    scores = (
        jnp.einsum("iqhe,ikhe->ihqk", query_four, key_four, preferred_element_type=jnp.float32)
        + key_mask
    )
    row_max = jnp.max(scores, axis=-1, keepdims=True)
    shifted = jnp.exp(scores - row_max)
    row_total = jnp.sum(shifted, axis=-1, keepdims=True)
    log_total = row_max + jnp.log(row_total)
    weights = (shifted / row_total).astype(jnp.bfloat16)
    mixed = jnp.einsum("ihqk,ikhe->iqhe", weights, value_four, preferred_element_type=jnp.float32)
    mixed = mixed.astype(jnp.bfloat16).reshape(group_rows, head_cols)
    regrouped = lax.all_to_all(mixed, "narrow", split_axis=0, concat_axis=1, tiled=True)
    middle = inputs + (jnp.dot(regrouped, full_out, preferred_element_type=jnp.float32) + b_out)
    normed2, unit2, inv2 = norm_parts(middle, ln2_gain, ln2_bias)
    normed2 = normed2.astype(jnp.bfloat16)
    up_rows = jnp.dot(normed2, full_up, preferred_element_type=jnp.float32) + full_up_bias.astype(
        jnp.float32
    )
    activated, gelu_back = jax.vjp(gelu_exact, up_rows)
    hidden = activated.astype(jnp.bfloat16)
    layer_out = middle + jnp.dot(hidden, full_down, preferred_element_type=jnp.float32) + b_down
    grad_float = cotangent.astype(jnp.float32)
    grad_hidden = contract_cols(cotangent, full_down)
    grad_up = gelu_back(grad_hidden)[0].astype(jnp.bfloat16)
    grad_normed2 = contract_cols(grad_up, full_up)
    grad_norm_two, gain2_grad, bias2_grad = norm_back(grad_normed2, unit2, inv2, ln2_gain)
    grad_middle = grad_float + grad_norm_two
    grad_branch = grad_middle.astype(jnp.bfloat16)
    grad_mixed = contract_cols(grad_branch, full_out).astype(jnp.bfloat16)
    grad_heads = lax.all_to_all(grad_mixed, "narrow", split_axis=1, concat_axis=0, tiled=True)
    grad_four = grad_heads.reshape(shaped)
    scores_again = (
        jnp.einsum("iqhe,ikhe->ihqk", query_four, key_four, preferred_element_type=jnp.float32)
        + key_mask
    )
    prob_rows = jnp.exp(scores_again - log_total)
    weights_again = prob_rows.astype(jnp.bfloat16)
    grad_values = jnp.einsum(
        "ihqk,iqhe->ikhe", weights_again, grad_four, preferred_element_type=jnp.float32
    ).astype(jnp.bfloat16)
    grad_probs = jnp.einsum(
        "iqhe,ikhe->ihqk", grad_four, value_four, preferred_element_type=jnp.float32
    )
    grad_scores = (
        prob_rows * (grad_probs - jnp.sum(grad_probs * prob_rows, axis=-1, keepdims=True))
    ).astype(jnp.bfloat16)
    grad_queries = jnp.einsum(
        "ihqk,ikhe->iqhe", grad_scores, key_four, preferred_element_type=jnp.float32
    ).astype(jnp.bfloat16)
    grad_keys = jnp.einsum(
        "ihqk,iqhe->ikhe", grad_scores, query_four, preferred_element_type=jnp.float32
    ).astype(jnp.bfloat16)
    grad_queries = grad_queries.reshape(group_rows, head_cols) * 0.125
    grad_keys = grad_keys.reshape(group_rows, head_cols)
    grad_values = grad_values.reshape(group_rows, head_cols)
    grad_qkv = jnp.stack([grad_queries, grad_keys, grad_values], axis=1)
    w_qkv_grad = jnp.einsum("td,tcf->dcf", grouped, grad_qkv, preferred_element_type=jnp.float32)
    b_qv_grad = jnp.stack(
        [
            jnp.sum(grad_queries.astype(jnp.float32), axis=0),
            jnp.sum(grad_values.astype(jnp.float32), axis=0),
        ]
    )
    full_qkv = lax.all_gather(w_qkv, "narrow", axis=2, tiled=True)
    grad_qkv_own = lax.all_to_all(grad_qkv, "narrow", split_axis=0, concat_axis=2, tiled=True)
    grad_normed1 = jnp.einsum(
        "tcf,dcf->td", grad_qkv_own, full_qkv, preferred_element_type=jnp.float32
    )
    grad_norm_one, gain1_grad, bias1_grad = norm_back(grad_normed1, unit1, inv1, ln1_gain)
    input_grad = grad_middle + grad_norm_one
    out_bias_grad = jnp.sum(grad_branch.astype(jnp.float32), axis=0)
    down_bias_grad = jnp.sum(grad_float, axis=0)
    up_bias_full = jnp.sum(grad_up.astype(jnp.float32), axis=0, keepdims=True)
    out_whole = contract_rows(regrouped, grad_branch)
    down_whole = contract_rows(hidden, cotangent)
    out_part, down_part = (
        lax.psum_scatter(
            out_whole.astype(jnp.bfloat16), "narrow", scatter_dimension=0, tiled=True
        ).astype(jnp.float32),
        lax.psum_scatter(
            down_whole.astype(jnp.bfloat16), "narrow", scatter_dimension=0, tiled=True
        ).astype(jnp.float32),
    )
    up_whole = contract_rows(normed2, grad_up)
    up_part = lax.psum_scatter(
        up_whole.astype(jnp.bfloat16), "narrow", scatter_dimension=1, tiled=True
    ).astype(jnp.float32)
    summed = lax.psum((w_qkv_grad, b_qv_grad, out_part, up_part, down_part), "wide")
    small = lax.psum(
        (
            gain1_grad,
            bias1_grad,
            out_bias_grad,
            gain2_grad,
            bias2_grad,
            down_bias_grad,
            up_bias_full,
        ),
        ("wide", "narrow"),
    )
    shard_cols = b_up.shape[1]
    up_bias_grad = lax.dynamic_slice_in_dim(
        small[6], lax.axis_index("narrow") * shard_cols, shard_cols, 1
    )
    return (
        layer_out,
        input_grad,
        small[0],
        small[1],
        summed[0],
        summed[1],
        summed[2],
        small[2],
        small[3],
        small[4],
        summed[3],
        up_bias_grad,
        summed[4],
        small[5],
    )


def solution(mesh):
    placed = (
        P(("wide", "narrow"), None),
        P("wide"),
        P(),
        P(),
        P(None, None, "narrow"),
        P(None, "narrow"),
        P("narrow", None),
        P(),
        P(),
        P(),
        P(None, "narrow"),
        P(None, "narrow"),
        P("narrow", None),
        P(),
        P(("wide", "narrow"), None),
    )
    return jax.shard_map(
        on_device,
        mesh=mesh,
        in_specs=placed,
        out_specs=(
            P(("wide", "narrow"), None),
            P(("wide", "narrow"), None),
            P(),
            P(),
            P(None, None, "narrow"),
            P(None, "narrow"),
            P("narrow", None),
            P(),
            P(),
            P(),
            P(None, "narrow"),
            P(None, "narrow"),
            P("narrow", None),
            P(),
        ),
        check_vma=False,
    )
```

profile of v0, /device:TPU:8, one launch (start us, length us, event | category | flops | bytes accessed | tf_op | source)
XLA Modules:
  0.0 723.6 jit_solution(6485242681903960717)
XLA Ops:
  16.6 38.9 %all-gather.6.cloned.1.call-done = bf16[3360,768]{1,0:T(8,128)(2,1)} async-done(((bf16[840,768]{1,0:T(8,128)(2,1)}), bf16[3360,768]{1,0:T(8,128)(2,1)}) %all-gather.6.cloned.1.call-update) | async-done | bytes 5160976 | tf_op jit(solution)/shard_map/all_gather | solution.py:69
  55.5 5.5 fusion.47
  65.0 5.4 squeeze.8
  87.6 6.3 add_reduce_fusion
  100.1 5.6 convert_bitcast_fusion.2
  117.5 29.0 %all_gather.21 = bf16[1,3072]{1,0:T(2,128)(2,1)S(1)} all-gather(bf16[1,768]{1,0:T(2,128)(2,1)S(1)} %copy-done.34), channel_id=1, replica_groups=mesh['wide'=8,'narrow'=4] {'narrow'}, dimensions={1}, use_global_device_ids=true | all-gather | bytes 7680 | tf_op jit(solution)/shard_map/all_gather | solution.py:76
  151.9 11.5 %fusion.43 = f32[840,3072]{1,0:T(8,128)} fusion(bf16[768,3072]{1,0:T(8,128)(2,1)} %all-gather.10.cloned.1.call-done, f32[840,768]{1,0:T(8,128)} %copy-done.8, f32[768]{0:T(1024)S(1)} %copy-done.38, f32[768]{0:T(1024)S(1)} %copy-done.33, f32[840]{0:T(1024)S(1)} %add_rsqrt_fusion, f32[840]{0:T(1024)S(1)} %broadcast_multiply_fusion.4), kind=kOutput, calls=%fused_computation.104 | convolution fusion | flops 3966842880 | bytes 17633856 | tf_op jit(solution)/shard_map/dot_general | solution.py:108
  163.4 31.9 %convert_reduce_fusion = (f32[3072]{0:T(1024)S(1)}, bf16[840,3072]{1,0:T(8,128)(2,1)S(1)}, f32[840,3072]{1,0:T(8,128)}) fusion(f32[840,3072]{1,0:T(8,128)} %fusion.43, f32[3072]{0:T(1024)S(1)} %bitcast.79, bf16[840,768]{1,0:T(8,128)(2,1)S(1)} %copy-done.17, bf16[3072,768]{1,0:T(8,128)(2,1)} %all-gather.12.cloned.1.call-done), kind=kOutput, calls=%fused_computation.9 | convolution fusion | flops 4157150208 | bytes 31838208 | tf_op jit(solution)/shard_map/dot_general | solution.py:40
  204.6 9.9 %convolution_convert_fusion.1 = bf16[768,3072]{1,0:T(8,128)(2,1)} fusion(bf16[840,3072]{1,0:T(8,128)(2,1)} %copy-done.42, f32[840,768]{1,0:T(8,128)} %copy-done.8, f32[768]{0:T(1024)S(1)} %copy-done.39, f32[768]{0:T(1024)S(1)} %copy-done.33, f32[840]{0:T(1024)S(1)} %add_rsqrt_fusion, f32[840]{0:T(1024)S(1)} %broadcast_multiply_fusion.4), kind=kOutput, calls=%fused_computation.31 | convolution fusion | flops 3969202176 | bytes 12472896 | tf_op jit(solution)/shard_map/dot_general | solution.py:34
  225.2 12.0 %multiply_convert_fusion.1 = bf16[840,3072]{1,0:T(8,128)(2,1)} fusion(f32[840,3072]{1,0:T(8,128)} %get-tuple-element.37, f32[840,3072]{1,0:T(8,128)} %fusion.43, f32[3072]{0:T(1024)S(1)} %bitcast.80), kind=kLoop, calls=%fused_computation.11 | loop fusion | flops 10321920 | bytes 25817088 | tf_op jit(solution)/shard_map/convert_element_type | solution.py:112
  237.1 10.3 %convolution_convert_fusion = bf16[3072,768]{1,0:T(8,128)(2,1)} fusion(bf16[840,3072]{1,0:T(8,128)(2,1)} %multiply_convert_fusion.1, bf16[840,768]{1,0:T(8,128)(2,1)S(1)} %copy-done.19), kind=kOutput, calls=%fused_computation.30 | convolution fusion | flops 3965976576 | bytes 11169792 | tf_op jit(solution)/shard_map/dot_general | solution.py:34
  253.5 16.3 %multiply_reduce_fusion = (f32[12,3,280]{2,1,0:T(4,128)S(1)}, f32[12,3,280,280]{2,3,1,0:T(8,128)}) fusion(f32[12,3,280,280]{2,3,1,0:T(8,128)} %copy-done, f32[12,3,280]{2,1,0:T(4,128)S(1)} %log_add_fusion, f32[12,280]{1,0:T(8,128)S(1)} %copy-done.22, bf16[12,280,3,64]{1,0,3,2:T(8,128)(2,1)} %add_convert_fusion.1, bf16[12,280,3,64]{1,0,3,2:T(8,128)(2,1)S(1)} %reshape.150), kind=kOutput, calls=%fused_computation.2 | convolution fusion | flops 372546720 | bytes 25253760 | tf_op jit(solution)/shard_map/iqhe,ikhe->ihqk/dot_general | solution.py:133
  269.9 13.6 %multiply_convert_fusion = bf16[12,3,280,280]{2,3,1,0:T(8,128)(2,1)S(1)} fusion(f32[12,3,280,280]{2,3,1,0:T(8,128)} %get-tuple-element.49, f32[12,3,280,280]{2,3,1,0:T(8,128)} %copy-done, f32[12,3,280]{2,1,0:T(4,128)S(1)} %get-tuple-element.48, f32[12,3,280]{2,1,0:T(4,128)S(1)} %log_add_fusion, f32[12,280]{1,0:T(8,128)S(1)} %copy-done.22), kind=kLoop, calls=%fused_computation.1 | loop fusion | flops 14112000 | bytes 28318080 | tf_op jit(solution)/shard_map/convert_element_type | solution.py:138
  293.8 6.6 convert_bitcast_fusion.1
  307.3 7.3 %convert_reduce_fusion.2 = (f32[3,64]{1,0:T(4,128)S(1)}, bf16[12,280,3,64]{1,3,2,0:T(8,128)(2,1)S(1)}) fusion(f32[12,3,280,280]{2,3,1,0:T(8,128)} %copy-done, f32[12,3,280]{2,1,0:T(4,128)S(1)} %log_add_fusion, f32[12,280]{1,0:T(8,128)S(1)} %copy-done.22, bf16[12,280,3,64]{1,0,3,2:T(8,128)(2,1)S(1)} %reshape.150), kind=kOutput, calls=%fused_computation.37 | convolution fusion | flops 371669568 | bytes 13924608 | tf_op jit(solution)/shard_map/ihqk,iqhe->ikhe/dot_general | solution.py:130
  323.4 11.3 %copy.78 = bf16[3360,3,192]{2,1,0:T(4,128)(2,1)} copy(bf16[3360,3,192]{0,2,1:T(8,128)(2,1)} %constant_dynamic-update-slice_fusion) | data formatting | bytes 7741440 | tf_op jit(solution)/shard_map/stack | solution.py:148
  334.7 5.8 all-to-all-start.2
  340.9 9.5 %add_add_fusion = f32[840,768]{1,0:T(8,128)} fusion(f32[840,768]{1,0:T(8,128)S(1)} %copy-done.10, bf16[840,3072]{1,0:T(8,128)(2,1)} %multiply_convert_fusion.1, bf16[3072,768]{1,0:T(8,128)(2,1)} %all-gather.12.cloned.1.call-done, f32[768]{0:T(1024)S(1)} %copy-done.40), kind=kOutput, calls=%fused_computation.61 | convolution fusion | flops 3964907520 | bytes 15043584 | tf_op jit(solution)/shard_map/dot_general | solution.py:113
  350.6 8.2 %fusion.48 = f32[768,576]{0,1} fusion(bf16[3360,576]{0,1:T(8,128)(2,1)} %bitcast.15, bf16[3360,768]{1,0:T(8,128)(2,1)} %all-gather.6.cloned.1.call-done), kind=kOutput, calls=%fused_computation.108 | convolution fusion | flops 2972712960 | bytes 10801152
  358.9 78.5 %all-to-all-done.2 = bf16[3360,3,192]{2,1,0:T(4,128)(2,1)} async-done(((bf16[3360,3,192]{2,1,0:T(4,128)(2,1)}), bf16[3360,3,192]{2,1,0:T(4,128)(2,1)}, u32[]{:S(2)}, u32[]{:S(2)}) %all-to-all-start.2) | async-done | bytes 3870752 | tf_op jit(solution)/shard_map/all_to_all | solution.py:157
  437.5 11.4 %copy.79 = bf16[4,840,3,192]{1,3,0,2:T(8,128)(2,1)} copy(bf16[4,840,3,192]{3,2,1,0:T(4,128)(2,1)} %bitcast.11) | data formatting | bytes 7741440 | tf_op jit(solution)/shard_map/all_to_all | solution.py:157
  448.8 8.6 %fusion.25 = (f32[768]{0:T(1024)S(1)}, f32[840]{0:T(1024)S(1)}, f32[840]{0:T(1024)S(1)}, f32[768]{0:T(1024)S(1)}, f32[840,768,1]{1,0,2:T(8,128)}) fusion(bf16[840,768]{1,0:T(8,128)(2,1)S(1)} %copy-done.3, f32[840]{0:T(1024)S(1)} %copy-done.31, f32[840]{0:T(1024)S(1)} %copy-done.29, f32[768]{0:T(1024)S(1)} %copy-done.32, bf16[840,3,768]{0,2,1:T(8,128)(2,1)} %bitcast.74, ...), kind=kOutput, calls=%fused_computation.54 | convolution fusion | flops 2979161088 | bytes 11303040 | tf_op jit(solution)/shard_map/tcf,dcf->td/dot_general | solution.py:158
  457.4 41.6 %all-reduce = (f32[768]{0:T(1024)}, f32[768]{0:T(1024)}, f32[768]{0:T(1024)}, f32[768]{0:T(1024)}, f32[768]{0:T(1024)}, /*index=5*/f32[1,3072]{1,0:T(1,128)S(1)}, f32[768]{0:T(1024)}) all-reduce(f32[768]{0:T(1024)S(1)} %get-tuple-element.16, f32[768]{0:T(1024)S(1)} %get-tuple-element.21, ...), channel_id=1, replica_groups=mesh['wide'=8,'narrow'=4] {'wide','narrow'}, use_global_device_ids=true, to_apply=%region_12.13 | all-reduce | flops 7680 | bytes 61440 | tf_op jit(solution)/shard_map/psum | solution.py:181
  503.6 210.2 %all-reduce.6 = (f32[2,192]{1,0:T(2,128)}, f32[192,768]{1,0:T(8,128)}, f32[768,768]{1,0:T(8,128)}, f32[768,768]{1,0:T(8,128)}) all-reduce(f32[2,192]{1,0:T(2,128)S(1)} %pad_maximum_fusion, bf16[192,768]{1,0:T(8,128)(2,1)S(1)} %copy-done.27, ...), channel_id=1, replica_groups=mesh['wide'=8,'narrow'=4] {'wide'}, use_global_device_ids=true, to_apply=%region_18.19 | all-reduce | flops 1327488 | bytes 7965696 | tf_op jit(solution)/shard_map/psum | solution.py:180
  (168 shorter events, 113.3 us)
Async XLA Ops:
  7.2 48.3 %all-gather.6.cloned.1.call-start = ((), (), s32[]{:S(2)}) async-start(), calls=%async_computation.6 | async-start | bytes 6451200 | tf_op jit(solution)/shard_map/all_gather | solution.py:69
  10.7 44.9 %copy-start.20 = (bf16[768,3,192]{0,2,1:T(8,128)(2,1)S(1)}, bf16[768,3,192]{0,2,1:T(8,128)(2,1)}, u32[]{:S(2)}) copy-start(bf16[768,3,192]{0,2,1:T(8,128)(2,1)} %param.19) | copy-start | bytes 2654212
  14.2 132.4 %all-gather.8.cloned.1.call-start = ((), (), s32[]{:S(2)}) async-start(), calls=%async_computation.7 | async-start | bytes 1474560 | tf_op jit(solution)/shard_map/all_gather | solution.py:71
  15.0 136.9 %all-gather.10.cloned.1.call-start = ((), (), s32[]{:S(2)}) async-start(), calls=%async_computation.8 | async-start | bytes 5898240 | tf_op jit(solution)/shard_map/all_gather | solution.py:75
  15.7 147.7 %all-gather.12.cloned.1.call-start = ((), (), s32[]{:S(2)}) async-start(), calls=%async_computation.9 | async-start | bytes 5898240 | tf_op jit(solution)/shard_map/all_gather | solution.py:72
  16.4 80.9 %copy-start.21 = (f32[12,280]{1,0:T(8,128)}, f32[12,280]{1,0:T(8,128)S(1)}, u32[]{:S(2)}) copy-start(f32[12,280]{1,0:T(8,128)S(1)} %fusion.40) | copy-start | bytes 40324
  111.2 35.4 %copy-start.2 = (bf16[840,768]{1,0:T(8,128)(2,1)S(1)}, bf16[840,768]{1,0:T(8,128)(2,1)}, u32[]{:S(2)}) copy-start(bf16[840,768]{1,0:T(8,128)(2,1)} %param.15) | copy-start | bytes 3870724
  111.3 35.4 %copy-start.37 = (f32[768]{0:T(1024)S(1)}, f32[768]{0:T(1024)}, u32[]{:S(2)}) copy-start(f32[768]{0:T(1024)} %param.22) | copy-start | bytes 9220
  113.9 32.7 %all-to-all-start = ((bf16[4,840,192]{1,2,0:T(8,128)(2,1)}), bf16[4,840,192]{1,2,0:T(8,128)(2,1)S(1)}, u32[]{:S(2)}, u32[]{:S(2)}) async-start(bf16[4,840,192]{1,2,0:T(8,128)(2,1)} %copy.64), calls=%async_computation | async-start | bytes 2752512 | tf_op jit(solution)/shard_map/all_to_all | solution.py:104
  117.5 241.4 %reduce-scatter.4.cloned.1.call-start = ((), (), s32[]{:S(2)}) async-start(), calls=%async_computation.12 | async-start | bytes 1474560 | tf_op jit(solution)/shard_map/reduce_scatter | solution.py:169
  151.9 11.5 %copy-start.17 = (bf16[840,768]{1,0:T(8,128)(2,1)S(1)}, bf16[840,768]{1,0:T(8,128)(2,1)}, u32[]{:S(2)}) copy-start(bf16[840,768]{1,0:T(8,128)(2,1)} %param.29) | copy-start | bytes 3870724
  163.4 31.9 %copy-start.9 = (f32[840,768]{1,0:T(8,128)S(1)}, f32[840,768]{1,0:T(8,128)}, u32[]{:S(2)}) copy-start(f32[840,768]{1,0:T(8,128)} %copy-done.8) | copy-start | bytes 7741444
  163.4 31.9 %copy-start.36 = (bf16[768,3072]{1,0:T(8,128)(2,1)S(1)}, bf16[768,3072]{1,0:T(8,128)(2,1)}, u32[]{:S(2)}) copy-start(bf16[768,3072]{1,0:T(8,128)(2,1)} %all-gather.10.cloned.1.call-done) | copy-start | bytes 14155780
  201.4 14.0 %copy-start.7 = (f32[840,768]{1,0:T(8,128)}, f32[840,768]{1,0:T(8,128)S(1)}, u32[]{:S(2)}) copy-start(f32[840,768]{1,0:T(8,128)S(1)} %get-tuple-element.39) | copy-start | bytes 7741444
  203.9 244.9 %all-gather.14.cloned.1.call-start = ((), (), s32[]{:S(2)}) async-start(), calls=%async_computation.10 | async-start | bytes 4423680 | tf_op jit(solution)/shard_map/all_gather | solution.py:156
  204.5 299.1 %reduce-scatter.6.cloned.1.call-start = ((), (), s32[]{:S(2)}) async-start(), calls=%async_computation.13 | async-start | bytes 5898240 | tf_op jit(solution)/shard_map/reduce_scatter | solution.py:177
  221.6 25.9 %all-to-all-start.1 = ((bf16[840,4,192]{0,2,1:T(8,128)(2,1)}), bf16[840,4,192]{0,2,1:T(8,128)(2,1)S(1)}, u32[]{:S(2)}, u32[]{:S(2)}) async-start(bf16[840,4,192]{0,2,1:T(8,128)(2,1)} %bitcast.6), calls=%async_computation.1 | async-start | bytes 2752512 | tf_op jit(solution)/shard_map/all_to_all | solution.py:122
  225.1 278.5 %reduce-scatter.8.cloned.1.call-start = ((), (), s32[]{:S(2)}) async-start(), calls=%async_computation.14 | async-start | bytes 5898240 | tf_op jit(solution)/shard_map/reduce_scatter | solution.py:172
  225.2 12.0 %copy-start.19 = (bf16[840,768]{1,0:T(8,128)(2,1)S(1)}, bf16[840,768]{1,0:T(8,128)(2,1)}, u32[]{:S(2)}) copy-start(bf16[840,768]{1,0:T(8,128)(2,1)} %param.29) | copy-start | bytes 3870724
  269.8 13.6 %copy-start.5 = (bf16[12,280,3,64]{1,0,3,2:T(8,128)(2,1)S(1)}, bf16[12,280,3,64]{1,0,3,2:T(8,128)(2,1)}, u32[]{:S(2)}) copy-start(bf16[12,280,3,64]{1,0,3,2:T(8,128)(2,1)} %copy-done.4) | copy-start | bytes 3870724
  334.7 102.7 %all-to-all-start.2 = ((bf16[3360,3,192]{2,1,0:T(4,128)(2,1)}), bf16[3360,3,192]{2,1,0:T(4,128)(2,1)}, u32[]{:S(2)}, u32[]{:S(2)}) async-start(bf16[3360,3,192]{2,1,0:T(4,128)(2,1)} %copy.78), calls=%async_computation.2 | async-start | bytes 13762560 | tf_op jit(solution)/shard_map/all_to_all | solution.py:157
  340.6 373.3 %all-reduce.5.cloned.1.call-start = ((), (), s32[]{:S(2)}) async-start(), calls=%async_computation.11 | async-start | bytes 3538944 | tf_op jit(solution)/shard_map/psum | solution.py:180
  437.5 11.4 %copy-start.31 = (f32[840]{0:T(1024)S(1)}, f32[840]{0:T(1024)}, u32[]{:S(2)}) copy-start(f32[840]{0:T(1024)} %copy-done.30) | copy-start | bytes 10084
  437.5 11.4 %copy-start.32 = (f32[768]{0:T(1024)S(1)}, f32[768]{0:T(1024)}, u32[]{:S(2)}) copy-start(f32[768]{0:T(1024)} %param.17) | copy-start | bytes 9220
  (31 other events, 144.6 us)
Sparse Core Ops, SparseCore 0:
  14.3 41.1 all-gather.5
  57.1 17.4 all-gather.7
  76.1 37.4 all-gather.9
  115.0 47.3 all-gather.11
  204.1 26.2 reduce-scatter.3
  231.9 32.1 all-gather.13
  266.8 47.8 reduce-scatter.5
  317.2 67.7 reduce-scatter.7
  389.6 94.5 all-reduce.4
where the time goes:
time: 738 us; the launch traced here: 724 us
  blocking collectives  281 us (38%)
  matrix products  154 us (21%)
  waiting for transfers between devices  120 us (16%)
  local copies, waits for them, and re-layouts  93.4 us (13%)
  other arithmetic  47.3 us (6%)
  between operations  14.9 us (2%)
  starting transfers between devices  13.5 us (2%)
    psum x1, blocking collectives, on_device(): lax.psum((w_qkv_grad, b_qv_grad, out_part, up_part, down_part), 'wide')  210 us
    all_to_all x1, waiting for transfers between devices, on_device(): lax.all_to_all(grad_qkv, 'narrow', split_axis=0, concat_axis=2, tiled=True)  78.5 us
    psum x1, blocking collectives, on_device(): lax.psum((gain1_grad, bias1_grad, out_bias_grad, gain2_grad, bias2_grad,...  41.6 us
    dot_general x3, matrix products, contract_cols(): lax.dot_general(left_side, right_side, (((1,), (1,)), ((), ())), preferre...  40.2 us
    all_gather x1, waiting for transfers between devices, on_device(): grouped = lax.all_gather(normed1, 'narrow', axis=0, tiled=True)  38.9 us
    all_gather x1, blocking collectives, on_device(): lax.all_gather(b_up, 'narrow', axis=1, tiled=True)  29 us
    dot_general x3, matrix products, contract_rows(): lax.dot_general(left_side, right_side, (((0,), (0,)), ((), ())), preferre...  22.7 us
    another operation x4, local copies, waits for them, and re-layouts, on_device(): grad_qkv = jnp.stack([grad_queries, grad_keys, grad_values], axis=1)  19.5 us
  transfers between devices with their start and end apart: 12, of which 2 were waited for; matrix products, arithmetic and copies ran while one was open for 32% of the time, Pallas kernels for 0%

commit v1 on v0

v1 whole, which is shorter than its diff:
```python
import functools

import jax
import jax.numpy as jnp
from jax import lax
from jax.experimental import pallas as pl
from jax.experimental.pallas import tpu as pltpu
from jax.sharding import PartitionSpec as P

HEAD = 64
WORDS = 40
PACK = 16
LANES = 128
BLOCK = 256

norm_eps = 1e-06
masked_value = -1000000000.0
bf = jnp.bfloat16
f32 = jnp.float32


def mul_nn(a, b):
    return lax.dot_general(a, b, (((1,), (0,)), ((), ())), preferred_element_type=f32)


def mul_nt(a, b):
    return lax.dot_general(a, b, (((1,), (1,)), ((), ())), preferred_element_type=f32)


def mul_tn(a, b):
    return lax.dot_general(a, b, (((0,), (0,)), ((), ())), preferred_element_type=f32)


def pad_rows(x, rows):
    if x.shape[0] == rows:
        return x
    return jnp.concatenate([x, jnp.zeros((rows - x.shape[0],) + x.shape[1:], x.dtype)], axis=0)


def unit_parts(x):
    centred = x - jnp.mean(x, axis=-1, keepdims=True)
    inv = lax.rsqrt(jnp.mean(centred * centred, axis=-1, keepdims=True) + norm_eps)
    return centred * inv, inv


def norm_back(grad, unit, inv, gain):
    scaled = grad * gain
    inner = (
        scaled
        - jnp.mean(scaled, axis=-1, keepdims=True)
        - unit * jnp.mean(scaled * unit, axis=-1, keepdims=True)
    )
    return inv * inner


def col_sum(x):
    return jnp.sum(x, axis=0, keepdims=True)


def full(shape):
    return pl.BlockSpec(shape, lambda *_: (0,) * len(shape))


def per_item(shape):
    return pl.BlockSpec((None,) + shape, lambda i, *_: (i,) + (0,) * len(shape))


def params(mib):
    return pltpu.CompilerParams(vmem_limit_bytes=mib << 20)


def attend_kernel(first, counts, tokens, gain, bias, w, b, *outs):
    if first:
        q_out, k_out, v_out, mixed_out, log_out, normed_out = outs
    else:
        q_out, k_out, v_out, mixed_out, log_out = outs
    rows, width = q_out.shape
    unit, _ = unit_parts(pad_rows(tokens[...].astype(f32), rows))
    normed = (unit * gain[...] + bias[...]).astype(bf)
    if first:
        normed_out[...] = normed
    q = ((mul_nt(normed, w[0]) + b[0:1]) * 0.125).astype(bf)
    k = mul_nt(normed, w[1]).astype(bf)
    v = (mul_nt(normed, w[2]) + b[1:2]).astype(bf)
    q_out[...] = q
    k_out[...] = k
    v_out[...] = v
    valid = WORDS + counts[pl.program_id(0)]
    mask = jnp.where(lax.broadcasted_iota(jnp.int32, (1, rows), 1) < valid, 0.0, masked_value)
    lane = lax.broadcasted_iota(jnp.int32, (rows, LANES), 1)
    low = lane < HEAD
    logs = jnp.zeros((rows, LANES), f32)
    for p in range(width // LANES):
        at = slice(p * LANES, (p + 1) * LANES)
        q_two, k_two, v_two = q[:, at], k[:, at], v[:, at]
        tops, sums = [], []
        for h in range(2):
            here = low if h == 0 else ~low
            scores = mul_nt(jnp.where(here, q_two, 0), k_two) + mask
            top = jnp.max(scores, axis=1, keepdims=True)
            shifted = jnp.exp(scores - top).astype(bf)
            sums.append(mul_nn(shifted, jnp.where(here, v_two, 1)))
            tops.append(top)
        total = pltpu.roll(jnp.where(low, sums[1], sums[0]), HEAD, 1)
        mixed_out[:, at] = (jnp.where(low, sums[0], sums[1]) / total).astype(bf)
        log_two = jnp.log(total)
        logs = jnp.where(lane == 2 * p, tops[0] + log_two[:, 0:1], logs)
        logs = jnp.where(lane == 2 * p + 1, tops[1] + log_two[:, HEAD : HEAD + 1], logs)
    log_out[...] = logs.T[: log_out.shape[0]]


def attend(first, counts, tokens, gain, bias, w, b, rows):
    items, _, dim = tokens.shape
    width = w.shape[1]
    wide_out = jax.ShapeDtypeStruct((items, rows, width), bf)
    outs = [wide_out] * 4 + [jax.ShapeDtypeStruct((items, 8, rows), f32)]
    specs = [per_item((rows, width))] * 4 + [per_item((8, rows))]
    if first:
        outs.append(jax.ShapeDtypeStruct((items, rows, dim), bf))
        specs.append(per_item((rows, dim)))
    return pl.pallas_call(
        functools.partial(attend_kernel, first),
        grid_spec=pltpu.PrefetchScalarGridSpec(
            num_scalar_prefetch=1,
            grid=(items,),
            in_specs=[
                per_item(tokens.shape[1:]),
                full((1, dim)),
                full((1, dim)),
                full(w.shape),
                full(b.shape),
            ],
            out_specs=specs,
        ),
        out_shape=outs,
        compiler_params=params(32),
        cost_estimate=pl.CostEstimate(
            flops=items * rows * (6 * dim * width + 24 * width // HEAD * LANES * rows),
            bytes_accessed=items * rows * (dim * 4 + width * 8) + w.size * 2,
            transcendentals=items * rows * rows * width // HEAD,
        ),
        name="attend",
    )(counts, tokens, gain, bias, w, b)


def branch_kernel(tokens, cot, mixed_a, mixed_b, w_a, w_b, b_out, gain, bias, middle_out, normed_out, cot_out):
    rows = normed_out.shape[0]
    middle = (
        pad_rows(tokens[...].astype(f32), rows)
        + (mul_nn(mixed_a[...], w_a[...]) + mul_nn(mixed_b[...], w_b[...]))
        + b_out[...]
    )
    middle_out[...] = middle
    unit, _ = unit_parts(middle)
    normed_out[...] = (unit * gain[...] + bias[...]).astype(bf)
    cot_out[...] = pad_rows(cot[...].astype(f32), rows).astype(bf)


def branch(tokens, cot, mixed_a, mixed_b, w_a, w_b, b_out, gain, bias):
    items, seq, dim = tokens.shape
    _, rows, width = mixed_a.shape
    return pl.pallas_call(
        branch_kernel,
        grid=(items,),
        in_specs=[per_item((seq, dim))] * 2
        + [per_item((rows, width))] * 2
        + [full(w_a.shape)] * 2
        + [full((1, dim))] * 3,
        out_specs=[per_item((rows, dim))] * 3,
        out_shape=[
            jax.ShapeDtypeStruct((items, rows, dim), f32),
            jax.ShapeDtypeStruct((items, rows, dim), bf),
            jax.ShapeDtypeStruct((items, rows, dim), bf),
        ],
        compiler_params=params(24),
        cost_estimate=pl.CostEstimate(
            flops=items * rows * 4 * dim * width,
            bytes_accessed=items * rows * dim * 16,
            transcendentals=items * rows,
        ),
        name="branch",
    )(tokens, cot, mixed_a, mixed_b, w_a, w_b, b_out, gain, bias)


def feed_kernel(
    last, per, normed, cot, base, base_grad, b_down, up_a, up_b, down_a, down_b, b_up,
    out_ref, grad_ref, dup_ref, ddown_ref, dbias_ref, hidden_ref, gu_ref, *scratch
):
    step = pl.program_id(0)
    items, rows, dim = normed.shape
    acc = scratch[0] if last else out_ref
    is_a = step < per

    @pl.when(step == 0)
    def _():
        if last:
            acc[...] = base[...]
            grad_ref[...] = base_grad[...]
        else:
            acc[...] = base[...] + b_down[...][None]
            grad_ref[...] = jnp.zeros_like(grad_ref)

    w_up = jnp.where(is_a, up_a[...], up_b[...])
    w_down = jnp.where(is_a, down_a[...], down_b[...])
    bias_sum = jnp.zeros((1, w_up.shape[1]), f32)
    for i in range(items):
        up = mul_nn(normed[i], w_up) + b_up[...]
        grad_hidden = mul_nt(cot[i], w_down)
        cdf = 0.5 * (1.0 + lax.erf(up * 0.7071067811865476))
        slope = cdf + up * (jnp.exp(-0.5 * up * up) * 0.3989422804014327)
        hidden = (up * cdf).astype(bf)
        gu = (slope * grad_hidden).astype(bf)
        hidden_ref[i] = hidden
        gu_ref[i] = gu
        bias_sum = bias_sum + col_sum(gu.astype(f32))
        acc[i] += mul_nn(hidden, w_down)
        grad_ref[i] += mul_nt(gu, w_up)
    dbias_ref[...] = bias_sum
    flat = (items * rows, dim)
    hidden = hidden_ref[...].reshape(items * rows, -1)
    gu = gu_ref[...].reshape(items * rows, -1)
    ddown_ref[...] = mul_tn(hidden, cot[...].reshape(flat)).astype(bf)
    dup_ref[...] = mul_tn(normed[...].reshape(flat), gu).astype(bf)
    if last:

        @pl.when(step == pl.num_programs(0) - 1)
        def _():
            for i in range(items):
                out_ref[i] = acc[i, : out_ref.shape[1]]


def feed(last, normed, cot, base, base_grad, b_down, up_a, up_b, down_a, down_b, b_up, seq):
    items, rows, dim = normed.shape
    units = up_a.shape[1]
    per = units // BLOCK
    steps = 2 * per
    out_rows = seq if last else rows
    full3 = full((items, rows, dim))
    if not last:
        base_grad = b_down
    scratch = [pltpu.VMEM((items, rows, BLOCK), bf)] * 2
    if last:
        scratch.append(pltpu.VMEM((items, rows, dim), f32))
    return pl.pallas_call(
        functools.partial(feed_kernel, last, per),
        grid=(steps,),
        in_specs=[
            full3,
            full3,
            full3,
            full3 if last else full((1, dim)),
            full((1, dim)),
            pl.BlockSpec((dim, BLOCK), lambda j: (0, jnp.minimum(j, per - 1))),
            pl.BlockSpec((dim, BLOCK), lambda j: (0, jnp.maximum(j - per, 0))),
            pl.BlockSpec((BLOCK, dim), lambda j: (jnp.minimum(j, per - 1), 0)),
            pl.BlockSpec((BLOCK, dim), lambda j: (jnp.maximum(j - per, 0), 0)),
            pl.BlockSpec((1, BLOCK), lambda j: (0, j)),
        ],
        out_specs=[
            full((items, out_rows, dim)),
            full3,
            pl.BlockSpec((None, dim, BLOCK), lambda j: (j // per, 0, j % per)),
            pl.BlockSpec((None, BLOCK, dim), lambda j: (j // per, j % per, 0)),
            pl.BlockSpec((1, BLOCK), lambda j: (0, j)),
        ],
        out_shape=[
            jax.ShapeDtypeStruct((items, out_rows, dim), f32),
            jax.ShapeDtypeStruct((items, rows, dim), f32),
            jax.ShapeDtypeStruct((2, dim, units), bf),
            jax.ShapeDtypeStruct((2, units, dim), bf),
            jax.ShapeDtypeStruct((1, 2 * units), f32),
        ],
        scratch_shapes=scratch,
        compiler_params=params(56),
        cost_estimate=pl.CostEstimate(
            flops=steps * items * rows * dim * BLOCK * 12,
            bytes_accessed=items * rows * dim * 20 + units * dim * 16,
            transcendentals=steps * items * rows * BLOCK * 2,
        ),
        name="feed",
    )(normed, cot, base, base_grad, b_down, up_a, up_b, down_a, down_b, b_up)


def unbranch_kernel(
    middle, cot, grad_in, gain, mixed_a, mixed_b, w_a, w_b,
    grad_out, gmix_a, gmix_b, dw_out, small, branch_ref
):
    step = pl.program_id(0)
    unit, inv = unit_parts(middle[...])
    grad = grad_in[...]
    cot_f = cot[...].astype(f32)
    grad_middle = cot_f + norm_back(grad, unit, inv, gain[...])
    grad_out[...] = grad_middle
    grad_branch = grad_middle.astype(bf)
    branch_ref[step] = grad_branch
    gmix_a[...] = mul_nt(grad_branch, w_a[...]).astype(bf)
    gmix_b[...] = mul_nt(grad_branch, w_b[...]).astype(bf)

    @pl.when(step == 0)
    def _():
        small[...] = jnp.zeros_like(small)

    small[0:1] += col_sum(grad * unit)
    small[1:2] += col_sum(grad)
    small[2:3] += col_sum(grad_branch.astype(f32))
    small[3:4] += col_sum(cot_f)

    @pl.when(step == pl.num_programs(0) - 1)
    def _():
        items, rows, dim = branch_ref.shape
        gb = branch_ref[...].reshape(items * rows, dim)
        width = mixed_a.shape[2]
        quarter = width // 2
        for n, mixed in ((0, mixed_a), (1, mixed_b)):
            dw = mul_tn(mixed[...].reshape(items * rows, width), gb).astype(bf)
            dw_out[2 * n] = dw[:quarter]
            dw_out[2 * n + 1] = dw[quarter:]


def unbranch(middle, cot, grad_in, gain, mixed_a, mixed_b, w_a, w_b):
    items, rows, dim = middle.shape
    width = mixed_a.shape[2]
    each = per_item((rows, dim))
    return pl.pallas_call(
        unbranch_kernel,
        grid=(items,),
        in_specs=[each, each, each, full((1, dim))]
        + [full(mixed_a.shape)] * 2
        + [full(w_a.shape)] * 2,
        out_specs=[
            each,
            per_item((rows, width)),
            per_item((rows, width)),
            full((4, width // 2, dim)),
            full((8, dim)),
        ],
        out_shape=[
            jax.ShapeDtypeStruct((items, rows, dim), f32),
            jax.ShapeDtypeStruct((items, rows, width), bf),
            jax.ShapeDtypeStruct((items, rows, width), bf),
            jax.ShapeDtypeStruct((4, width // 2, dim), bf),
            jax.ShapeDtypeStruct((8, dim), f32),
        ],
        scratch_shapes=[pltpu.VMEM((items, rows, dim), bf)],
        compiler_params=params(32),
        cost_estimate=pl.CostEstimate(
            flops=items * rows * 8 * dim * width,
            bytes_accessed=items * rows * dim * 20,
            transcendentals=items * rows,
        ),
        name="unbranch",
    )(middle, cot, grad_in, gain, mixed_a, mixed_b, w_a, w_b)


def unattend_kernel(final, counts, q, k, v, gmix, logs, normed, w, *refs):
    if final:
        grad_in, grad_middle, tokens, gain, x_out, dw_out, db_out, small, g_ref = refs
    else:
        x_out, dw_out, db_out, g_ref = refs
    step = pl.program_id(0)
    rows, width = q.shape
    valid = WORDS + counts[step]
    mask = jnp.where(lax.broadcasted_iota(jnp.int32, (rows, 1), 0) < valid, 0.0, masked_value)
    low = lax.broadcasted_iota(jnp.int32, (rows, LANES), 1) < HEAD
    for p in range(width // LANES):
        at = slice(p * LANES, (p + 1) * LANES)
        q_two, k_two, v_two, g_two = q[:, at], k[:, at], v[:, at], gmix[:, at]
        dq, dk, dv = [], [], []
        for h in range(2):
            here = low if h == 0 else ~low
            scores = mul_nt(jnp.where(here, k_two, 0), q_two) + mask
            prob = jnp.exp(scores - logs[2 * p + h : 2 * p + h + 1])
            grad_prob = mul_nt(jnp.where(here, v_two, 0), g_two)
            inner = jnp.sum(grad_prob * prob, axis=0, keepdims=True)
            grad_scores = (prob * (grad_prob - inner)).astype(bf)
            dv.append(mul_nn(prob.astype(bf), g_two))
            dk.append(mul_nn(grad_scores, q_two))
            dq.append(mul_tn(grad_scores, k_two))
        for c, pair in enumerate((dq, dk, dv)):
            merged = jnp.where(low, pair[0], pair[1]).astype(bf)
            if c == 0:
                merged = merged * jnp.asarray(0.125, bf)
            g_ref[step, :, c * width + p * LANES : c * width + (p + 1) * LANES] = merged
    g = g_ref[step]
    grad = mul_nn(g, w[...].reshape(3 * width, -1))

    @pl.when(step == 0)
    def _():
        db_out[...] = jnp.zeros_like(db_out)
        if final:
            small[...] = jnp.zeros_like(small)

    sums = col_sum(g.astype(f32))
    db_out[0:1] += sums[:, :width]
    db_out[1:2] += sums[:, 2 * width :]
    if final:
        grad = grad + grad_in[...]
        unit, inv = unit_parts(pad_rows(tokens[...].astype(f32), rows))
        small[0:1] += col_sum(grad * unit)
        small[1:2] += col_sum(grad)
        seq = x_out.shape[0]
        x_out[...] = (grad_middle[...] + norm_back(grad, unit, inv, gain[...]))[:seq]
    else:
        x_out[...] = grad

    @pl.when(step == pl.num_programs(0) - 1)
    def _():
        items = g_ref.shape[0]
        flat = normed[...].reshape(items * rows, -1)
        dw = mul_tn(g_ref[...].reshape(items * rows, 3 * width), flat).astype(bf)
        quarter = width // 2
        for c in range(3):
            dw_out[0, c] = dw[c * width : c * width + quarter]
            dw_out[1, c] = dw[c * width + quarter : (c + 1) * width]


def unattend(counts, q, k, v, gmix, logs, normed, w, rest=None):
    final = rest is not None
    items, rows, width = q.shape
    dim = normed.shape[2]
    wide = per_item((rows, width))
    specs = [wide] * 4 + [per_item((8, rows)), full(normed.shape), full(w.shape)]
    args = [counts, q, k, v, gmix, logs, normed, w]
    out_rows = rows
    extra_out, extra_spec = [], []
    if final:
        grad_in, grad_middle, tokens, gain = rest
        out_rows = tokens.shape[1]
        specs += [per_item((rows, dim))] * 2 + [per_item(tokens.shape[1:]), full((1, dim))]
        args += list(rest)
        extra_out, extra_spec = [jax.ShapeDtypeStruct((8, dim), f32)], [full((8, dim))]
    return pl.pallas_call(
        functools.partial(unattend_kernel, final),
        grid_spec=pltpu.PrefetchScalarGridSpec(
            num_scalar_prefetch=1,
            grid=(items,),
            in_specs=specs,
            out_specs=[
                per_item((out_rows, dim)),
                full((2, 3, width // 2, dim)),
                full((8, width)),
            ]
            + extra_spec,
            scratch_shapes=[pltpu.VMEM((items, rows, 3 * width), bf)],
        ),
        out_shape=[
            jax.ShapeDtypeStruct((items, out_rows, dim), f32),
            jax.ShapeDtypeStruct((2, 3, width // 2, dim), bf),
            jax.ShapeDtypeStruct((8, width), f32),
        ]
        + extra_out,
        compiler_params=params(40),
        cost_estimate=pl.CostEstimate(
            flops=items * rows * (12 * dim * width + 60 * width // HEAD * LANES * rows),
            bytes_accessed=items * rows * (dim * 8 + width * 8) + w.size * 4,
            transcendentals=items * rows * rows * width // HEAD,
        ),
        name="unattend",
    )(*args)


def exchange(x, axis, size, mask):
    return lax.ppermute(x, axis, [(i, i ^ mask) for i in range(size)])


def reduce_over(x, axis, size):
    masks = []
    mask = 1
    while mask < size:
        masks.append(mask)
        mask *= 2
    me = lax.axis_index(axis)
    for mask in masks:
        half = x.shape[0] // 2
        up = (me // mask) % 2
        sent = lax.dynamic_slice_in_dim(x, (1 - up) * half, half, 0)
        kept = lax.dynamic_slice_in_dim(x, up * half, half, 0)
        got = exchange(sent, axis, size, mask)
        x = (kept.astype(f32) + got.astype(f32)).astype(bf)
    for mask in reversed(masks):
        up = (me // mask) % 2
        got = exchange(x, axis, size, mask)
        first = jnp.where(up == 0, x, got)
        second = jnp.where(up == 0, got, x)
        x = jnp.concatenate([first, second], axis=0)
    return x


def add_bf(*parts):
    total = parts[0].astype(f32)
    for part in parts[1:]:
        total = total + part.astype(f32)
    return total.astype(bf)


def own_quarter(quarters, narrow):
    one = exchange(quarters[1], "narrow", narrow, 1)
    three = exchange(quarters[3], "narrow", narrow, 1)
    peer = exchange(add_bf(quarters[2], three), "narrow", narrow, 2)
    return add_bf(quarters[0], one, peer)


def on_device(
    wide,
    narrow,
    tokens,
    patch_counts,
    ln1_gain,
    ln1_bias,
    w_qkv,
    b_qv,
    w_out,
    b_out,
    ln2_gain,
    ln2_bias,
    w_up,
    b_up,
    w_down,
    b_down,
    cotangent,
):
    own_rows, dim = tokens.shape
    items = patch_counts.shape[0] // narrow
    seq = own_rows // items
    rows = -(-seq // PACK) * PACK
    heads = w_qkv.shape[2]
    units = w_up.shape[1]
    me = lax.axis_index("narrow")
    counts = lax.dynamic_slice_in_dim(patch_counts, me * items, items, 0)
    tokens3 = tokens.reshape(items, seq, dim)
    cot3 = cotangent.reshape(items, seq, dim)
    row = lambda x: x.reshape(1, dim)

    w_flat = w_qkv.transpose(1, 2, 0)
    small_in = jnp.concatenate(
        [
            jnp.pad(b_qv, ((0, 0), (0, dim - heads))),
            jnp.pad(b_up.astype(f32), ((0, 5), (0, dim - units))),
        ],
        axis=0,
    )

    def others(x):
        mate = exchange(x, "narrow", narrow, 1)
        peer = exchange(x, "narrow", narrow, 2)
        return x, mate, peer, exchange(peer, "narrow", narrow, 1)

    qkv4 = others(w_flat)
    out4 = others(w_out)
    small4 = others(small_in)
    up4 = others(w_up)
    down4 = others(w_down)

    def half(four, n, axis):
        return jnp.concatenate([four[2 * n], four[2 * n + 1]], axis=axis)

    w_half = [half(qkv4, n, 1) for n in range(2)]
    out_half = [half(out4, n, 0) for n in range(2)]
    b_half = [half([s[:2, :heads] for s in small4], n, 1) for n in range(2)]
    up_bias = [half([s[2:3, :units] for s in small4], n, 1) for n in range(2)]

    q_a, k_a, v_a, mixed_a, log_a, normed1 = attend(
        True, counts, tokens3, row(ln1_gain), row(ln1_bias), w_half[0], b_half[0], rows
    )
    q_b, k_b, v_b, mixed_b, log_b = attend(
        False, counts, tokens3, row(ln1_gain), row(ln1_bias), w_half[1], b_half[1], rows
    )
    middle, normed2, cot_pad = branch(
        tokens3, cot3, mixed_a, mixed_b, out_half[0], out_half[1], row(b_out), row(ln2_gain), row(ln2_bias)
    )
    part, grad_part, dup_a, ddown_a, dbias_a = feed(
        False, normed2, cot_pad, middle, None, row(b_down),
        up4[0], up4[1], down4[0], down4[1], up_bias[0], seq,
    )
    layer_out, grad_norm2, dup_b, ddown_b, dbias_b = feed(
        True, normed2, cot_pad, part, grad_part, row(b_down),
        up4[2], up4[3], down4[2], down4[3], up_bias[1], seq,
    )
    grad_middle, gmix_a, gmix_b, dw_out, small_two = unbranch(
        middle, cot_pad, grad_norm2, row(ln2_gain), mixed_a, mixed_b, out_half[0], out_half[1]
    )
    grad_one, dqkv_b, dbqv_b = unattend(counts, q_b, k_b, v_b, gmix_b, log_b, normed1, w_half[1])
    input_grad, dqkv_a, dbqv_a, small_one = unattend(
        counts, q_a, k_a, v_a, gmix_a, log_a, normed1, w_half[0],
        (grad_one, grad_middle, tokens3, row(ln1_gain)),
    )

    feed_quarters = [
        jnp.concatenate([du[n], dd[n]], axis=0)
        for du, dd in ((dup_a, ddown_a), (dup_b, ddown_b))
        for n in range(2)
    ]
    feed_sum = reduce_over(own_quarter(feed_quarters, narrow), "wide", wide)

    vectors = [small_one[0:1], small_one[1:2]] + [small_two[n : n + 1] for n in range(4)]
    quarters = []
    for n in range(4):
        dqkv, dbqv, dbias = ((dqkv_a, dbqv_a, dbias_a), (dqkv_b, dbqv_b, dbias_b))[n // 2]
        at = n % 2
        tail = vectors + [
            dbias[:, at * units : (at + 1) * units],
            jnp.pad(dbqv[0:2, at * heads : (at + 1) * heads], ((0, 0), (0, dim - heads))),
        ]
        tail = jnp.concatenate(tail, axis=0)
        total_rows = 4 * heads + tail.shape[0]
        pad = -total_rows % (8 * wide)
        tail = jnp.pad(tail, ((0, pad), (0, 0))).astype(bf)
        quarters.append(
            jnp.concatenate([dqkv[at].reshape(3 * heads, dim), dw_out[n], tail], axis=0)
        )
    rest_sum = reduce_over(own_quarter(quarters, narrow), "wide", wide).astype(f32)
    feed_sum = feed_sum.astype(f32)
    vec = rest_sum[4 * heads :]
    return (
        layer_out.reshape(own_rows, dim),
        input_grad.reshape(own_rows, dim),
        vec[0],
        vec[1],
        rest_sum[: 3 * heads].reshape(3, heads, dim).transpose(2, 0, 1),
        vec[7:9, :heads],
        rest_sum[3 * heads : 4 * heads],
        vec[4],
        vec[2],
        vec[3],
        feed_sum[:dim],
        vec[6:7, :units],
        feed_sum[dim:],
        vec[5],
    )


def solution(mesh):
    wide, narrow = mesh.shape["wide"], mesh.shape["narrow"]
    assert narrow == 4 and wide & (wide - 1) == 0
    rows = P(("wide", "narrow"), None)
    return jax.shard_map(
        functools.partial(on_device, wide, narrow),
        mesh=mesh,
        in_specs=(
            rows,
            P("wide"),
            P(),
            P(),
            P(None, None, "narrow"),
            P(None, "narrow"),
            P("narrow", None),
            P(),
            P(),
            P(),
            P(None, "narrow"),
            P(None, "narrow"),
            P("narrow", None),
            P(),
            rows,
        ),
        out_specs=(
            rows,
            rows,
            P(),
            P(),
            P(None, None, "narrow"),
            P(None, "narrow"),
            P("narrow", None),
            P(),
            P(),
            P(),
            P(None, "narrow"),
            P(None, "narrow"),
            P("narrow", None),
            P(),
        ),
        check_vma=False,
    )
```

time: 738 us -> 415 us (0.56); the launches traced: 724 us -> 411 us
  blocking collectives: 281 us -> 0 us
  matrix products: 154 us -> 0 us
  Pallas kernels: 0 us -> 106 us
  waiting for transfers between devices: 120 us -> 196 us
  local copies, waits for them, and re-layouts: 93.4 us -> 33.9 us
  starting transfers between devices: 13.5 us -> 44.8 us
  other arithmetic: 47.3 us -> 29.5 us
  between operations: 14.9 us -> 1.25 us
    psum x2 -> x0, blocking collectives: 252 us -> none  [the longest x1 210 us: on_device(): lax.psum((w_qkv_grad, b_qv_grad, out_part, up_part, down_part), 'wide')]
    ppermute x0 -> x33, waiting for transfers between devices: none -> 196 us  [exchange(): return lax.ppermute(x, axis, [(i, i ^ mask) for i in range(size)])]
    dot_general x16 -> x0, matrix products: 140 us -> none  [the longest x3 40.2 us: contract_cols(): lax.dot_general(left_side, right_side, (((1,), (1,)), ((), ())), preferre...]
    pallas_call x0 -> x8, Pallas kernels: none -> 106 us  [the longest x2 47.4 us: feed(): pl.pallas_call(functools.partial(feed_kernel, last, per), grid=(steps,),...]
    all_to_all x3 -> x0, waiting for transfers between devices: 78.6 us -> none  [the longest x1 78.5 us: on_device(): lax.all_to_all(grad_qkv, 'narrow', split_axis=0, concat_axis=2, tiled=True)]
    ppermute x0 -> x33, starting transfers between devices: none -> 44.8 us  [exchange(): return lax.ppermute(x, axis, [(i, i ^ mask) for i in range(size)])]
    all_gather x5 -> x0, waiting for transfers between devices: 39 us -> none  [the longest x1 38.9 us: on_device(): grouped = lax.all_gather(normed1, 'narrow', axis=0, tiled=True)]
    all_gather x1 -> x0, blocking collectives: 29 us -> none  [on_device(): lax.all_gather(b_up, 'narrow', axis=1, tiled=True)]
  transfers between devices with their start and end apart: 12 -> 33, of which waited for: 2 -> 16; matrix products, arithmetic and copies ran while one was open for 32% -> 11% of each run, Pallas kernels for 0% -> 26%
where the time goes in v1:
time: 415 us; the launch traced here: 411 us
  waiting for transfers between devices  196 us (47%)
  Pallas kernels  106 us (26%)
  starting transfers between devices  44.8 us (11%)
  local copies, waits for them, and re-layouts  33.9 us (8%)
  other arithmetic  29.5 us (7%)
    ppermute x33, waiting for transfers between devices, exchange(): return lax.ppermute(x, axis, [(i, i ^ mask) for i in range(size)])  196 us
    pallas_call x2, Pallas kernels, feed(): pl.pallas_call(functools.partial(feed_kernel, last, per), grid=(steps,),...  47.4 us
    ppermute x33, starting transfers between devices, exchange(): return lax.ppermute(x, axis, [(i, i ^ mask) for i in range(size)])  44.8 us
    pallas_call x2, Pallas kernels, unattend(): pl.pallas_call(functools.partial(unattend_kernel, final), grid_spec=pltpu...  29.8 us
    pallas_call x2, Pallas kernels, attend(): pl.pallas_call(functools.partial(attend_kernel, first), grid_spec=pltpu.P...  20.2 us
    unnamed x79, local copies, waits for them, and re-layouts  15.4 us
    convert_element_type x4, other arithmetic, add_bf(): return total.astype(bf)  9.38 us
  transfers between devices with their start and end apart: 33, of which 16 were waited for; matrix products, arithmetic and copies ran while one was open for 11% of the time, Pallas kernels for 26%

profile of v1, /device:TPU:8, one launch (start us, length us, event | category | flops | bytes accessed | tf_op | source)
XLA Modules:
  0.0 411.1 jit_solution(1674322216136953240)
XLA Ops:
  12.4 11.5 %collective-permute-done.4 = f32[8,768]{1,0:T(8,128)S(1)} collective-permute-done((f32[8,768]{1,0:T(8,128)S(1)}, f32[8,768]{1,0:T(8,128)S(1)}, u32[]{:S(2)}, u32[]{:S(2)}) %collective-permute-start.4) | collective-permute-done | bytes 24608 | tf_op jit(solution)/shard_map/ppermute | solution.py:463
  33.2 10.1 %attend.2 = (bf16[3,288,384]{2,1,0:T(8,128)(2,1)S(1)}, bf16[3,288,384]{2,1,0:T(8,128)(2,1)S(1)}, bf16[3,288,384]{2,1,0:T(8,128)(2,1)S(1)}, bf16[3,288,384]{2,1,0...) custom-call(s32[3]{0:T(128)S(1)} %dynamic_slice.39.counts, ...), custom_call_target="tpu_custom_call" | custom-call | flops 6115295232 | bytes 7077888 | tf_op jit(solution)/shard_map/attend/pallas_call | solution.py:121
  44.2 10.7 %collective-permute-done.11.up_a = bf16[768,768]{1,0:T(8,128)(2,1)} collective-permute-done((bf16[768,768]{1,0:T(8,128)(2,1)}, bf16[768,768]{1,0:T(8,128)(2,1)}, u32[]{:S(2)}, u32[]{:S(2)}) %collective-permute-start.11) | collective-permute-done | bytes 1179680 | tf_op jit(solution)/shard_map/ppermute | solution.py:463
  54.9 24.9 %collective-permute-done.13.down_a = bf16[768,768]{1,0:T(8,128)(2,1)} collective-permute-done((bf16[768,768]{1,0:T(8,128)(2,1)}, bf16[768,768]{1,0:T(8,128)(2,1)}, u32[]{:S(2)}, u32[]{:S(2)}) %collective-permute-start.13) | collective-permute-done | bytes 1179680 | tf_op jit(solution)/shard_map/ppermute | solution.py:463
  79.9 10.1 %attend.3 = (bf16[3,288,384]{2,1,0:T(8,128)(2,1)S(1)}, bf16[3,288,384]{2,1,0:T(8,128)(2,1)S(1)}, bf16[3,288,384]{2,1,0:T(8,128)(2,1)S(1)}, bf16[3,288,384]{2,1,0:T(8,128)(2,1)S(1)}, f32[3,8,288]{2,1,0:T(8,128)S(1)}) custom-call(s32[3]{0:T(128)S(1)} %dynamic_slice.39.counts, bf16[3,280,768]{2,1,0:T(8,128)(2,1)S(1)} %bitcast.38, ...), custom_call_target="tpu_custom_call" | custom-call | flops 6115295232 | bytes 7077888 | tf_op jit(solution)/shard_map/attend/pallas_call | solution.py:121
  98.5 22.6 %feed.2 = (f32[3,288,768]{2,1,0:T(8,128)}, f32[3,288,768]{2,1,0:T(8,128)}, bf16[2,768,768]{2,1,0:T(8,128)(2,1)}, bf16[2,768,768]{2,1,0:T(8,128)(2,1)}, f32[1,1536]{1,0:T(1,128)}) custom-call(bf16[3,288,768]{2,1,0:T(8,128)(2,1)} %copy-done.12, bf16[3,288,768]{2,1,0:T(8,128)(2,1)} %copy-done.3, f32[3,288,768]{2,1,0:T(8,128)} %copy-done, ...), custom_call_target="tpu_custom_call" | custom-call | flops 12230590464 | bytes 22708224 | tf_op jit(solution)/shard_map/feed/pallas_call | solution.py:244
  121.7 4.0 slice_bitcast_fusion.6
  127.8 24.8 %feed.3 = (f32[3,280,768]{2,1,0:T(8,128)}, f32[3,288,768]{2,1,0:T(8,128)}, bf16[2,768,768]{2,1,0:T(8,128)(2,1)}, bf16[2,768,768]{2,1,0:T(8,128)(2,1)}, f32[1,1536]{1,0:T(1,128)}) custom-call(bf16[3,288,768]{2,1,0:T(8,128)(2,1)} %copy-done.12, bf16[3,288,768]{2,1,0:T(8,128)(2,1)} %copy-done.3, f32[3,288,768]{2,1,0:T(8,128)} %get-tuple-element.55.base, ...), custom_call_target="tpu_custom_call" | custom-call | flops 12230590464 | bytes 22708224 | tf_op jit(solution)/shard_map/feed/pallas_call | solution.py:244
  155.7 5.9 %unbranch.1 = (f32[3,288,768]{2,1,0:T(8,128)S(1)}, bf16[3,288,384]{2,1,0:T(8,128)(2,1)S(1)}, bf16[3,288,384]{2,1,0:T(8,128)(2,1)S(1)}, bf16[4,192,768]{2,1,0:T(8,128)(2,1)S(1)}, f32[8,768]{1,0:T(8,128)S(1)}) custom-call(f32[3,288,768]{2,1,0:T(8,128)S(1)} %copy-done.1, bf16[3,288,768]{2,1,0:T(8,128)(2,1)S(1)} %copy-done.4, f32[3,288,768]{2,1,0:T(8,128)S(1)} %copy-done.2, ...), custom_call_target="tpu_custom_call" | custom-call | flops 2038431744 | bytes 13271040 | tf_op jit(solution)/shard_map/unbranch/pallas_call | solution.py:324
  166.2 13.4 %unattend.2 = (f32[3,288,768]{2,1,0:T(8,128)S(1)}, bf16[2,3,192,768]{3,2,1,0:T(8,128)(2,1)S(1)}, f32[8,384]{1,0:T(8,128)S(1)}) custom-call(s32[3]{0:T(128)S(1)} %dynamic_slice.39.counts, bf16[3,288,384]{2,1,0:T(8,128)(2,1)S(1)} %copy-done.20, bf16[3,288,384]{2,1,0:T(8,128)(2,1)S(1)} %copy-done.22, bf16[3,288,384]{2,1,0:T(8,128)(2,1)S(1)} %copy-done.24, ...), custom_call_target="tpu_custom_call" | custom-call | flops 14523826176 | bytes 11501568 | tf_op jit(solution)/shard_map/unattend/pallas_call | solution.py:432
  179.7 16.4 %unattend.3 = (f32[3,280,768]{2,1,0:T(8,128)}, bf16[2,3,192,768]{3,2,1,0:T(8,128)(2,1)S(1)}, f32[8,384]{1,0:T(8,128)S(1)}, f32[8,768]{1,0:T(8,128)S(1)}) custom-call(s32[3]{0:T(128)S(1)} %dynamic_slice.39.counts, bf16[3,288,384]{2,1,0:T(8,128)(2,1)S(1)} %get-tuple-element.58.q, bf16[3,288,384]{2,1,0:T(8,128)(2,1)S(1)} %copy-done.16, ...), custom_call_target="tpu_custom_call" | custom-call | flops 14523826176 | bytes 11501568 | tf_op jit(solution)/shard_map/unattend/pallas_call | solution.py:432
  206.7 46.9 %collective-permute-done.26 = bf16[1536,768]{1,0:T(8,128)(2,1)} collective-permute-done((bf16[1536,768]{1,0:T(8,128)(2,1)S(1)}, bf16[1536,768]{1,0:T(8,128)(2,1)}, u32[]{:S(2)}, u32[]{:S(2)}) %collective-permute-start.26) | collective-permute-done | bytes 2359328 | tf_op jit(solution)/shard_map/ppermute | solution.py:463
  258.8 21.2 %collective-permute-done.17 = bf16[832,768]{1,0:T(8,128)(2,1)} collective-permute-done((bf16[832,768]{1,0:T(8,128)(2,1)}, bf16[832,768]{1,0:T(8,128)(2,1)}, u32[]{:S(2)}, u32[]{:S(2)}) %collective-permute-start.17) | collective-permute-done | bytes 1277984 | tf_op jit(solution)/shard_map/ppermute | solution.py:463
  285.6 14.3 %collective-permute-done.18 = bf16[416,768]{1,0:T(8,128)(2,1)} collective-permute-done((bf16[416,768]{1,0:T(8,128)(2,1)}, bf16[416,768]{1,0:T(8,128)(2,1)}, u32[]{:S(2)}, u32[]{:S(2)}) %collective-permute-start.18) | collective-permute-done | bytes 639008 | tf_op jit(solution)/shard_map/ppermute | solution.py:463
  305.8 7.1 %collective-permute-done.19 = bf16[208,768]{1,0:T(8,128)(2,1)} collective-permute-done((bf16[208,768]{1,0:T(8,128)(2,1)}, bf16[208,768]{1,0:T(8,128)(2,1)}, u32[]{:S(2)}, u32[]{:S(2)}) %collective-permute-start.19) | collective-permute-done | bytes 319520 | tf_op jit(solution)/shard_map/ppermute | solution.py:463
  314.1 4.4 %collective-permute-start.20 = (bf16[104,768]{1,0:T(8,128)(2,1)S(1)}, bf16[104,768]{1,0:T(8,128)(2,1)S(1)}, u32[]{:S(2)}, u32[]{:S(2)}) collective-permute-start(bf16[104,768]{1,0:T(8,128)(2,1)S(1)} %constant_dynamic-slice_fusion.3), channel_id=1, source_target_pairs={{0,16},{4,20},{8,24},{12,28},{16,0},{20,4},{24,8},{28,12},{1,17},{... | collective-permute-start | bytes 479240 | tf_op jit(solution)/shard_map/ppermute | solution.py:463
  318.5 5.9 %collective-permute-done.28 = bf16[384,768]{1,0:T(8,128)(2,1)S(1)} collective-permute-done((bf16[384,768]{1,0:T(8,128)(2,1)S(1)}, bf16[384,768]{1,0:T(8,128)(2,1)S(1)}, u32[]{:S(2)}, u32[]{:S(2)}) %collective-permute-start.28) | collective-permute-done | bytes 589856 | tf_op jit(solution)/shard_map/ppermute | solution.py:463
  324.6 4.4 %collective-permute-start.29 = (bf16[192,768]{1,0:T(8,128)(2,1)S(1)}, bf16[192,768]{1,0:T(8,128)(2,1)S(1)}, u32[]{:S(2)}, u32[]{:S(2)}) collective-permute-start(bf16[192,768]{1,0:T(8,128)(2,1)S(1)} %constant_dynamic-slice_fusion), channel_id=1, source_target_pairs={{0,16},{4,20},{8,24},{12,28},{16,0},{20,4},{24,8},{28,12},{1,17},{... | collective-permute-start | bytes 884744 | tf_op jit(solution)/shard_map/ppermute | solution.py:463
  329.1 12.1 %collective-permute-done.29 = bf16[192,768]{1,0:T(8,128)(2,1)S(1)} collective-permute-done((bf16[192,768]{1,0:T(8,128)(2,1)S(1)}, bf16[192,768]{1,0:T(8,128)(2,1)S(1)}, u32[]{:S(2)}, u32[]{:S(2)}) %collective-permute-start.29) | collective-permute-done | bytes 294944 | tf_op jit(solution)/shard_map/ppermute | solution.py:463
  344.8 9.8 %collective-permute-start.22 = (bf16[208,768]{1,0:T(8,128)(2,1)S(1)}, bf16[208,768]{1,0:T(8,128)(2,1)S(1)}, u32[]{:S(2)}, u32[]{:S(2)}) collective-permute-start(bf16[208,768]{1,0:T(8,128)(2,1)S(1)} %pad_maximum_fusion.6), channel_id=1, source_target_pairs={{0,8},{4,12},{8,0},{12,4},{16,24},{20,28},{24,16},{28,20},{1,9},{5... | collective-permute-start | bytes 958472 | tf_op jit(solution)/shard_map/ppermute | solution.py:463
  357.4 3.5 collective-permute-start.31
  360.9 4.2 %collective-permute-done.22 = bf16[208,768]{1,0:T(8,128)(2,1)S(1)} collective-permute-done((bf16[208,768]{1,0:T(8,128)(2,1)S(1)}, bf16[208,768]{1,0:T(8,128)(2,1)S(1)}, u32[]{:S(2)}, u32[]{:S(2)}) %collective-permute-start.22) | collective-permute-done | bytes 319520 | tf_op jit(solution)/shard_map/ppermute | solution.py:463
  367.6 10.1 %collective-permute-done.31 = bf16[384,768]{1,0:T(8,128)(2,1)S(1)} collective-permute-done((bf16[384,768]{1,0:T(8,128)(2,1)S(1)}, bf16[384,768]{1,0:T(8,128)(2,1)S(1)}, u32[]{:S(2)}, u32[]{:S(2)}) %collective-permute-start.31) | collective-permute-done | bytes 589856 | tf_op jit(solution)/shard_map/ppermute | solution.py:463
  388.8 19.0 %collective-permute-done.32 = bf16[768,768]{1,0:T(8,128)(2,1)S(1)} collective-permute-done((bf16[768,768]{1,0:T(8,128)(2,1)}, bf16[768,768]{1,0:T(8,128)(2,1)S(1)}, u32[]{:S(2)}, u32[]{:S(2)}) %collective-permute-start.32) | collective-permute-done | bytes 1179680 | tf_op jit(solution)/shard_map/ppermute | solution.py:463
  (204 shorter events, 92.7 us)
Async XLA Ops:
  0.6 30.9 %collective-permute-start.2 = (bf16[3,192,768]{2,1,0:T(8,128)(2,1)}, bf16[3,192,768]{2,1,0:T(8,128)(2,1)S(1)}, u32[]{:S(2)}, u32[]{:S(2)}) collective-permute-start(bf16[3,192,768]{2,1,0:T(8,128)(2,1)} %bitcast.46), channel_id=1, source_target_pairs={{0,2},{1,3},{2,0},{3,1},{4,6},{5,7},{6,4},{7,5},{8,10},{9,11},{10,... | collective-permute-start | bytes 2654216 | tf_op jit(solution)/shard_map/ppermute | solution.py:463
  2.2 29.7 %collective-permute-start = (bf16[3,192,768]{2,1,0:T(8,128)(2,1)}, bf16[3,192,768]{2,1,0:T(8,128)(2,1)S(1)}, u32[]{:S(2)}, u32[]{:S(2)}) collective-permute-start(bf16[3,192,768]{2,1,0:T(8,128)(2,1)} %bitcast.47), channel_id=1, source_target_pairs={{0,1},{1,0},{2,3},{3,2},{4,5},{5,4},{6,7},{7,6},{8,9},{9,8},{10,11... | collective-permute-start | bytes 2654216 | tf_op jit(solution)/shard_map/ppermute | solution.py:463
  3.6 20.4 %collective-permute-start.4 = (f32[8,768]{1,0:T(8,128)S(1)}, f32[8,768]{1,0:T(8,128)S(1)}, u32[]{:S(2)}, u32[]{:S(2)}) collective-permute-start(f32[8,768]{1,0:T(8,128)S(1)} %select_maximum_fusion), channel_id=1, source_target_pairs={{0,2},{1,3},{2,0},{3,1},{4,6},{5,7},{6,4},{7,5},{8,10},{9,11},{10,... | collective-permute-start | bytes 73736 | tf_op jit(solution)/shard_map/ppermute | solution.py:463
  4.4 25.1 %collective-permute-start.7 = (bf16[192,768]{1,0:T(8,128)(2,1)}, bf16[192,768]{1,0:T(8,128)(2,1)S(1)}, u32[]{:S(2)}, u32[]{:S(2)}) collective-permute-start(bf16[192,768]{1,0:T(8,128)(2,1)} %param.21), channel_id=1, source_target_pairs={{0,2},{1,3},{2,0},{3,1},{4,6},{5,7},{6,4},{7,5},{8,10},{9,11},{10,... | collective-permute-start | bytes 884744 | tf_op jit(solution)/shard_map/ppermute | solution.py:463
  12.4 17.2 %collective-permute-start.6 = (bf16[192,768]{1,0:T(8,128)(2,1)}, bf16[192,768]{1,0:T(8,128)(2,1)S(1)}, u32[]{:S(2)}, u32[]{:S(2)}) collective-permute-start(bf16[192,768]{1,0:T(8,128)(2,1)} %param.21), channel_id=1, source_target_pairs={{0,1},{1,0},{2,3},{3,2},{4,5},{5,4},{6,7},{7,6},{8,9},{9,8},{10,11... | collective-permute-start | bytes 884744 | tf_op jit(solution)/shard_map/ppermute | solution.py:463
  25.4 29.5 %collective-permute-start.11 = (bf16[768,768]{1,0:T(8,128)(2,1)}, bf16[768,768]{1,0:T(8,128)(2,1)}, u32[]{:S(2)}, u32[]{:S(2)}) collective-permute-start(bf16[768,768]{1,0:T(8,128)(2,1)} %up_a.1), channel_id=1, source_target_pairs={{0,2},{1,3},{2,0},{3,1},{4,6},{5,7},{6,4},{7,5},{8,10},{9,11},{10,... | collective-permute-start | bytes 3538952 | tf_op jit(solution)/shard_map/ppermute | solution.py:463
  29.6 50.2 %collective-permute-start.13 = (bf16[768,768]{1,0:T(8,128)(2,1)}, bf16[768,768]{1,0:T(8,128)(2,1)}, u32[]{:S(2)}, u32[]{:S(2)}) collective-permute-start(bf16[768,768]{1,0:T(8,128)(2,1)} %down_a.1), channel_id=1, source_target_pairs={{0,2},{1,3},{2,0},{3,1},{4,6},{5,7},{6,4},{7,5},{8,10},{9,11},{10,... | collective-permute-start | bytes 3538952 | tf_op jit(solution)/shard_map/ppermute | solution.py:463
  31.2 65.2 %collective-permute-start.10 = (bf16[768,768]{1,0:T(8,128)(2,1)}, bf16[768,768]{1,0:T(8,128)(2,1)S(1)}, u32[]{:S(2)}, u32[]{:S(2)}) collective-permute-start(bf16[768,768]{1,0:T(8,128)(2,1)} %down_a.1), channel_id=1, source_target_pairs={{0,1},{1,0},{2,3},{3,2},{4,5},{5,4},{6,7},{7,6},{8,9},{9,8},{10,11... | collective-permute-start | bytes 3538952 | tf_op jit(solution)/shard_map/ppermute | solution.py:463
  31.5 48.3 %collective-permute-start.3 = (bf16[3,192,768]{2,1,0:T(8,128)(2,1)S(1)}, bf16[3,192,768]{2,1,0:T(8,128)(2,1)S(1)}, u32[]{:S(2)}, u32[]{:S(2)}) collective-permute-start(bf16[3,192,768]{2,1,0:T(8,128)(2,1)S(1)} %collective-permute-done.2), channel_id=1, source_target_pairs={{0,1},{1,0},{2,3},{3,2},{4,5},{5,4},{6,7},{7,6},{8,9},{9,8},{10,11... | collective-permute-start | bytes 2654216 | tf_op jit(solution)/shard_map/ppermute | solution.py:463
  31.9 64.5 %collective-permute-start.9 = (bf16[768,768]{1,0:T(8,128)(2,1)S(1)}, bf16[768,768]{1,0:T(8,128)(2,1)S(1)}, u32[]{:S(2)}, u32[]{:S(2)}) collective-permute-start(bf16[768,768]{1,0:T(8,128)(2,1)S(1)} %copy-done.35), channel_id=1, source_target_pairs={{0,1},{1,0},{2,3},{3,2},{4,5},{5,4},{6,7},{7,6},{8,9},{9,8},{10,11... | collective-permute-start | bytes 3538952 | tf_op jit(solution)/shard_map/ppermute | solution.py:463
  54.9 72.9 %collective-permute-start.12 = (bf16[768,768]{1,0:T(8,128)(2,1)}, bf16[768,768]{1,0:T(8,128)(2,1)}, u32[]{:S(2)}, u32[]{:S(2)}) collective-permute-start(bf16[768,768]{1,0:T(8,128)(2,1)} %collective-permute-done.11.up_a), channel_id=1, source_target_pairs={{0,1},{1,0},{2,3},{3,2},{4,5},{5,4},{6,7},{7,6},{8,9},{9,8},{10,11... | collective-permute-start | bytes 3538952 | tf_op jit(solution)/shard_map/ppermute | solution.py:463
  79.8 48.0 %collective-permute-start.14 = (bf16[768,768]{1,0:T(8,128)(2,1)}, bf16[768,768]{1,0:T(8,128)(2,1)}, u32[]{:S(2)}, u32[]{:S(2)}) collective-permute-start(bf16[768,768]{1,0:T(8,128)(2,1)} %collective-permute-done.13.down_a), channel_id=1, source_target_pairs={{0,1},{1,0},{2,3},{3,2},{4,5},{5,4},{6,7},{7,6},{8,9},{9,8},{10,11... | collective-permute-start | bytes 3538952 | tf_op jit(solution)/shard_map/ppermute | solution.py:463
  127.3 79.4 %collective-permute-start.24 = (bf16[1536,768]{1,0:T(8,128)(2,1)}, bf16[1536,768]{1,0:T(8,128)(2,1)}, u32[]{:S(2)}, u32[]{:S(2)}) collective-permute-start(bf16[1536,768]{1,0:T(8,128)(2,1)} %pad_maximum_fusion), channel_id=1, source_target_pairs={{0,1},{1,0},{2,3},{3,2},{4,5},{5,4},{6,7},{7,6},{8,9},{9,8},{10,11... | collective-permute-start | bytes 7077896 | tf_op jit(solution)/shard_map/ppermute | solution.py:463
  164.7 32.3 %collective-permute-start.25 = (bf16[1536,768]{1,0:T(8,128)(2,1)}, bf16[1536,768]{1,0:T(8,128)(2,1)}, u32[]{:S(2)}, u32[]{:S(2)}) collective-permute-start(bf16[1536,768]{1,0:T(8,128)(2,1)} %pad_maximum_fusion.1), channel_id=1, source_target_pairs={{0,1},{1,0},{2,3},{3,2},{4,5},{5,4},{6,7},{7,6},{8,9},{9,8},{10,11... | collective-permute-start | bytes 7077896 | tf_op jit(solution)/shard_map/ppermute | solution.py:463
  199.3 54.3 %collective-permute-start.26 = (bf16[1536,768]{1,0:T(8,128)(2,1)S(1)}, bf16[1536,768]{1,0:T(8,128)(2,1)}, u32[]{:S(2)}, u32[]{:S(2)}) collective-permute-start(bf16[1536,768]{1,0:T(8,128)(2,1)S(1)} %add_convert_fusion.1), channel_id=1, source_target_pairs={{0,2},{1,3},{2,0},{3,1},{4,6},{5,7},{6,4},{7,5},{8,10},{9,11},{10,... | collective-permute-start | bytes 7077896 | tf_op jit(solution)/shard_map/ppermute | solution.py:463
  204.0 54.8 %collective-permute-start.15 = (bf16[832,768]{1,0:T(8,128)(2,1)}, bf16[832,768]{1,0:T(8,128)(2,1)}, u32[]{:S(2)}, u32[]{:S(2)}) collective-permute-start(bf16[832,768]{1,0:T(8,128)(2,1)} %fusion.5), channel_id=1, source_target_pairs={{0,1},{1,0},{2,3},{3,2},{4,5},{5,4},{6,7},{7,6},{8,9},{9,8},{10,11... | collective-permute-start | bytes 3833864 | tf_op jit(solution)/shard_map/ppermute | solution.py:463
  206.2 73.8 %collective-permute-start.17 = (bf16[832,768]{1,0:T(8,128)(2,1)}, bf16[832,768]{1,0:T(8,128)(2,1)}, u32[]{:S(2)}, u32[]{:S(2)}) collective-permute-start(bf16[832,768]{1,0:T(8,128)(2,1)} %add_convert_fusion.3), channel_id=1, source_target_pairs={{0,2},{1,3},{2,0},{3,1},{4,6},{5,7},{6,4},{7,5},{8,10},{9,11},{10,... | collective-permute-start | bytes 3833864 | tf_op jit(solution)/shard_map/ppermute | solution.py:463
  257.3 45.1 %collective-permute-start.27 = (bf16[768,768]{1,0:T(8,128)(2,1)S(1)}, bf16[768,768]{1,0:T(8,128)(2,1)}, u32[]{:S(2)}, u32[]{:S(2)}) collective-permute-start(bf16[768,768]{1,0:T(8,128)(2,1)S(1)} %constant_dynamic-slice_fusion.2), channel_id=1, source_target_pairs={{0,4},{4,0},{8,12},{12,8},{16,20},{20,16},{24,28},{28,24},{1,5},{5... | collective-permute-start | bytes 3538952 | tf_op jit(solution)/shard_map/ppermute | solution.py:463
  304.0 20.4 %collective-permute-start.28 = (bf16[384,768]{1,0:T(8,128)(2,1)S(1)}, bf16[384,768]{1,0:T(8,128)(2,1)S(1)}, u32[]{:S(2)}, u32[]{:S(2)}) collective-permute-start(bf16[384,768]{1,0:T(8,128)(2,1)S(1)} %constant_dynamic-slice_fusion.1), channel_id=1, source_target_pairs={{0,8},{4,12},{8,0},{12,4},{16,24},{20,28},{24,16},{28,20},{1,9},{5... | collective-permute-start | bytes 1769480 | tf_op jit(solution)/shard_map/ppermute | solution.py:463
  324.6 16.6 %collective-permute-start.29 = (bf16[192,768]{1,0:T(8,128)(2,1)S(1)}, bf16[192,768]{1,0:T(8,128)(2,1)S(1)}, u32[]{:S(2)}, u32[]{:S(2)}) collective-permute-start(bf16[192,768]{1,0:T(8,128)(2,1)S(1)} %constant_dynamic-slice_fusion), channel_id=1, source_target_pairs={{0,16},{4,20},{8,24},{12,28},{16,0},{20,4},{24,8},{28,12},{1,17},{... | collective-permute-start | bytes 884744 | tf_op jit(solution)/shard_map/ppermute | solution.py:463
  344.8 20.3 %collective-permute-start.22 = (bf16[208,768]{1,0:T(8,128)(2,1)S(1)}, bf16[208,768]{1,0:T(8,128)(2,1)S(1)}, u32[]{:S(2)}, u32[]{:S(2)}) collective-permute-start(bf16[208,768]{1,0:T(8,128)(2,1)S(1)} %pad_maximum_fusion.6), channel_id=1, source_target_pairs={{0,8},{4,12},{8,0},{12,4},{16,24},{20,28},{24,16},{28,20},{1,9},{5... | collective-permute-start | bytes 958472 | tf_op jit(solution)/shard_map/ppermute | solution.py:463
  357.4 20.3 %collective-permute-start.31 = (bf16[384,768]{1,0:T(8,128)(2,1)S(1)}, bf16[384,768]{1,0:T(8,128)(2,1)S(1)}, u32[]{:S(2)}, u32[]{:S(2)}) collective-permute-start(bf16[384,768]{1,0:T(8,128)(2,1)S(1)} %pad_maximum_fusion.5), channel_id=1, source_target_pairs={{0,8},{4,12},{8,0},{12,4},{16,24},{20,28},{24,16},{28,20},{1,9},{5... | collective-permute-start | bytes 1769480 | tf_op jit(solution)/shard_map/ppermute | solution.py:463
  366.1 17.2 %collective-permute-start.23 = (bf16[416,768]{1,0:T(8,128)(2,1)}, bf16[416,768]{1,0:T(8,128)(2,1)}, u32[]{:S(2)}, u32[]{:S(2)}) collective-permute-start(bf16[416,768]{1,0:T(8,128)(2,1)} %pad_maximum_fusion.4), channel_id=1, source_target_pairs={{0,4},{4,0},{8,12},{12,8},{16,20},{20,16},{24,28},{28,24},{1,5},{5... | collective-permute-start | bytes 1916936 | tf_op jit(solution)/shard_map/ppermute | solution.py:463
  379.0 28.9 %collective-permute-start.32 = (bf16[768,768]{1,0:T(8,128)(2,1)}, bf16[768,768]{1,0:T(8,128)(2,1)S(1)}, u32[]{:S(2)}, u32[]{:S(2)}) collective-permute-start(bf16[768,768]{1,0:T(8,128)(2,1)} %pad_maximum_fusion.3), channel_id=1, source_target_pairs={{0,4},{4,0},{8,12},{12,8},{16,20},{20,16},{24,28},{28,24},{1,5},{5... | collective-permute-start | bytes 3538952 | tf_op jit(solution)/shard_map/ppermute | solution.py:463
  (47 other events, 462.6 us)

commit v2 on v1

--- a/solution.py
+++ b/solution.py
@@ -63,6 +63,13 @@
 
 def per_item(shape):
     return pl.BlockSpec((None,) + shape, lambda i, *_: (i,) + (0,) * len(shape))
+
+
+TIMES = {"attend": 10, "branch": 3, "feed": 24, "unbranch": 6, "unattend": 13, "outer": 3}
+
+
+def lasting(us):
+    return pl.CostEstimate(flops=int(us * 1.15e9), bytes_accessed=0, transcendentals=0)
 
 
 def params(mib):
@@ -134,11 +141,7 @@
         ),
         out_shape=outs,
         compiler_params=params(32),
-        cost_estimate=pl.CostEstimate(
-            flops=items * rows * (6 * dim * width + 24 * width // HEAD * LANES * rows),
-            bytes_accessed=items * rows * (dim * 4 + width * 8) + w.size * 2,
-            transcendentals=items * rows * rows * width // HEAD,
-        ),
+        cost_estimate=lasting(TIMES["attend"]),
         name="attend",
     )(counts, tokens, gain, bias, w, b)
 
@@ -173,19 +176,17 @@
             jax.ShapeDtypeStruct((items, rows, dim), bf),
         ],
         compiler_params=params(24),
-        cost_estimate=pl.CostEstimate(
-            flops=items * rows * 4 * dim * width,
-            bytes_accessed=items * rows * dim * 16,
-            transcendentals=items * rows,
-        ),
+        cost_estimate=lasting(TIMES["branch"]),
         name="branch",
     )(tokens, cot, mixed_a, mixed_b, w_a, w_b, b_out, gain, bias)
 
 
-def feed_kernel(
-    last, per, normed, cot, base, base_grad, b_down, up_a, up_b, down_a, down_b, b_up,
-    out_ref, grad_ref, dup_ref, ddown_ref, dbias_ref, hidden_ref, gu_ref, *scratch
-):
+def feed_kernel(last, per, low_half, normed, cot, base, base_grad, b_down, *refs):
+    n_weights = 8 if last else 4
+    weights, (b_up, out_ref, grad_ref, dup_ref, ddown_ref, dbias_ref, hidden_ref, gu_ref, *scratch) = (
+        refs[:n_weights],
+        refs[n_weights:],
+    )
     step = pl.program_id(0)
     items, rows, dim = normed.shape
     acc = scratch[0] if last else out_ref
@@ -200,8 +201,25 @@
             acc[...] = base[...] + b_down[...][None]
             grad_ref[...] = jnp.zeros_like(grad_ref)
 
-    w_up = jnp.where(is_a, up_a[...], up_b[...])
-    w_down = jnp.where(is_a, down_a[...], down_b[...])
+    if last:
+        up_a, up_b, up_c, up_d, down_a, down_b, down_c, down_d = weights
+        is_low = low_half[0] == 0
+
+        def joined(first, second, axis):
+            low = jnp.where(is_low, first, second)
+            high = jnp.where(is_low, second, first)
+            return jnp.concatenate([low, high], axis=axis)
+
+        w_up = joined(
+            jnp.where(is_a, up_a[...], up_c[...]), jnp.where(is_a, up_b[...], up_d[...]), 0
+        )
+        w_down = joined(
+            jnp.where(is_a, down_a[...], down_c[...]), jnp.where(is_a, down_b[...], down_d[...]), 1
+        )
+    else:
+        up_a, up_c, down_a, down_c = weights
+        w_up = jnp.where(is_a, up_a[...], up_c[...])
+        w_down = jnp.where(is_a, down_a[...], down_c[...])
     bias_sum = jnp.zeros((1, w_up.shape[1]), f32)
     for i in range(items):
         up = mul_nn(normed[i], w_up) + b_up[...]
@@ -229,9 +247,9 @@
                 out_ref[i] = acc[i, : out_ref.shape[1]]
 
 
-def feed(last, normed, cot, base, base_grad, b_down, up_a, up_b, down_a, down_b, b_up, seq):
+def feed(last, low_half, normed, cot, base, base_grad, b_down, ups, downs, b_up, seq):
     items, rows, dim = normed.shape
-    units = up_a.shape[1]
+    units = ups[0].shape[1]
     per = units // BLOCK
     steps = 2 * per
     out_rows = seq if last else rows
@@ -241,28 +259,36 @@
     scratch = [pltpu.VMEM((items, rows, BLOCK), bf)] * 2
     if last:
         scratch.append(pltpu.VMEM((items, rows, dim), f32))
+    part = dim // (len(ups) // 2)
+    half = len(ups) // 2
+    first = lambda j: jnp.minimum(j, per - 1)
+    second = lambda j: jnp.maximum(j - per, 0)
     return pl.pallas_call(
         functools.partial(feed_kernel, last, per),
-        grid=(steps,),
-        in_specs=[
-            full3,
-            full3,
-            full3,
-            full3 if last else full((1, dim)),
-            full((1, dim)),
-            pl.BlockSpec((dim, BLOCK), lambda j: (0, jnp.minimum(j, per - 1))),
-            pl.BlockSpec((dim, BLOCK), lambda j: (0, jnp.maximum(j - per, 0))),
-            pl.BlockSpec((BLOCK, dim), lambda j: (jnp.minimum(j, per - 1), 0)),
-            pl.BlockSpec((BLOCK, dim), lambda j: (jnp.maximum(j - per, 0), 0)),
-            pl.BlockSpec((1, BLOCK), lambda j: (0, j)),
-        ],
-        out_specs=[
-            full((items, out_rows, dim)),
-            full3,
-            pl.BlockSpec((None, dim, BLOCK), lambda j: (j // per, 0, j % per)),
-            pl.BlockSpec((None, BLOCK, dim), lambda j: (j // per, j % per, 0)),
-            pl.BlockSpec((1, BLOCK), lambda j: (0, j)),
-        ],
+        grid_spec=pltpu.PrefetchScalarGridSpec(
+            num_scalar_prefetch=1,
+            grid=(steps,),
+            in_specs=[
+                full3,
+                full3,
+                full3,
+                full3 if last else full((1, dim)),
+                full((1, dim)),
+            ]
+            + [pl.BlockSpec((part, BLOCK), lambda j, *_: (0, first(j)))] * half
+            + [pl.BlockSpec((part, BLOCK), lambda j, *_: (0, second(j)))] * half
+            + [pl.BlockSpec((BLOCK, part), lambda j, *_: (first(j), 0))] * half
+            + [pl.BlockSpec((BLOCK, part), lambda j, *_: (second(j), 0))] * half
+            + [pl.BlockSpec((1, BLOCK), lambda j, *_: (0, j))],
+            out_specs=[
+                full((items, out_rows, dim)),
+                full3,
+                pl.BlockSpec((None, dim, BLOCK), lambda j, *_: (j // per, 0, j % per)),
+                pl.BlockSpec((None, BLOCK, dim), lambda j, *_: (j // per, j % per, 0)),
+                pl.BlockSpec((1, BLOCK), lambda j, *_: (0, j)),
+            ],
+            scratch_shapes=scratch,
+        ),
         out_shape=[
             jax.ShapeDtypeStruct((items, out_rows, dim), f32),
             jax.ShapeDtypeStruct((items, rows, dim), f32),
@@ -270,15 +296,10 @@
             jax.ShapeDtypeStruct((2, units, dim), bf),
             jax.ShapeDtypeStruct((1, 2 * units), f32),
         ],
-        scratch_shapes=scratch,
         compiler_params=params(56),
-        cost_estimate=pl.CostEstimate(
-            flops=steps * items * rows * dim * BLOCK * 12,
-            bytes_accessed=items * rows * dim * 20 + units * dim * 16,
-            transcendentals=steps * items * rows * BLOCK * 2,
-        ),
+        cost_estimate=lasting(TIMES["feed"]),
         name="feed",
-    )(normed, cot, base, base_grad, b_down, up_a, up_b, down_a, down_b, b_up)
+    )(low_half, normed, cot, base, base_grad, b_down, *ups, *downs, b_up)
 
 
 def unbranch_kernel(
@@ -343,20 +364,16 @@
         ],
         scratch_shapes=[pltpu.VMEM((items, rows, dim), bf)],
         compiler_params=params(32),
-        cost_estimate=pl.CostEstimate(
-            flops=items * rows * 8 * dim * width,
-            bytes_accessed=items * rows * dim * 20,
-            transcendentals=items * rows,
-        ),
+        cost_estimate=lasting(TIMES["unbranch"]),
         name="unbranch",
     )(middle, cot, grad_in, gain, mixed_a, mixed_b, w_a, w_b)
 
 
-def unattend_kernel(final, counts, q, k, v, gmix, logs, normed, w, *refs):
+def unattend_kernel(final, counts, q, k, v, gmix, logs, w, *refs):
     if final:
-        grad_in, grad_middle, tokens, gain, x_out, dw_out, db_out, small, g_ref = refs
+        grad_in, grad_middle, tokens, gain, x_out, g_ref, db_out, small = refs
     else:
-        x_out, dw_out, db_out, g_ref = refs
+        x_out, g_ref, db_out = refs
     step = pl.program_id(0)
     rows, width = q.shape
     valid = WORDS + counts[step]
@@ -380,8 +397,8 @@
             merged = jnp.where(low, pair[0], pair[1]).astype(bf)
             if c == 0:
                 merged = merged * jnp.asarray(0.125, bf)
-            g_ref[step, :, c * width + p * LANES : c * width + (p + 1) * LANES] = merged
-    g = g_ref[step]
+            g_ref[:, c * width + p * LANES : c * width + (p + 1) * LANES] = merged
+    g = g_ref[...]
     grad = mul_nn(g, w[...].reshape(3 * width, -1))
 
     @pl.when(step == 0)
@@ -403,24 +420,14 @@
     else:
         x_out[...] = grad
 
-    @pl.when(step == pl.num_programs(0) - 1)
-    def _():
-        items = g_ref.shape[0]
-        flat = normed[...].reshape(items * rows, -1)
-        dw = mul_tn(g_ref[...].reshape(items * rows, 3 * width), flat).astype(bf)
-        quarter = width // 2
-        for c in range(3):
-            dw_out[0, c] = dw[c * width : c * width + quarter]
-            dw_out[1, c] = dw[c * width + quarter : (c + 1) * width]
-
-
-def unattend(counts, q, k, v, gmix, logs, normed, w, rest=None):
+
+def unattend(counts, q, k, v, gmix, logs, w, rest=None):
     final = rest is not None
     items, rows, width = q.shape
-    dim = normed.shape[2]
+    dim = w.shape[2]
     wide = per_item((rows, width))
-    specs = [wide] * 4 + [per_item((8, rows)), full(normed.shape), full(w.shape)]
-    args = [counts, q, k, v, gmix, logs, normed, w]
+    specs = [wide] * 4 + [per_item((8, rows)), full(w.shape)]
+    args = [counts, q, k, v, gmix, logs, w]
     out_rows = rows
     extra_out, extra_spec = [], []
     if final:
@@ -437,53 +444,53 @@
             in_specs=specs,
             out_specs=[
                 per_item((out_rows, dim)),
-                full((2, 3, width // 2, dim)),
+                per_item((rows, 3 * width)),
                 full((8, width)),
             ]
             + extra_spec,
-            scratch_shapes=[pltpu.VMEM((items, rows, 3 * width), bf)],
         ),
         out_shape=[
             jax.ShapeDtypeStruct((items, out_rows, dim), f32),
-            jax.ShapeDtypeStruct((2, 3, width // 2, dim), bf),
+            jax.ShapeDtypeStruct((items, rows, 3 * width), bf),
             jax.ShapeDtypeStruct((8, width), f32),
         ]
         + extra_out,
         compiler_params=params(40),
-        cost_estimate=pl.CostEstimate(
-            flops=items * rows * (12 * dim * width + 60 * width // HEAD * LANES * rows),
-            bytes_accessed=items * rows * (dim * 8 + width * 8) + w.size * 4,
-            transcendentals=items * rows * rows * width // HEAD,
-        ),
+        cost_estimate=lasting(TIMES["unattend"]),
         name="unattend",
     )(*args)
 
 
+def outer_kernel(g, normed, dw_out):
+    items, rows, dim = normed.shape
+    dw = mul_tn(g[...].reshape(items * rows, -1), normed[...].reshape(items * rows, dim)).astype(bf)
+    quarter = dw.shape[0] // 2
+    dw_out[0] = dw[:quarter]
+    dw_out[1] = dw[quarter:]
+
+
+def outer(g, normed):
+    items, rows, width3 = g.shape
+    dim = normed.shape[2]
+    width = width3 // 3
+    return pl.pallas_call(
+        outer_kernel,
+        grid=(3,),
+        in_specs=[pl.BlockSpec((items, rows, width), lambda c: (0, 0, c)), full(normed.shape)],
+        out_specs=pl.BlockSpec((2, None, width // 2, dim), lambda c: (0, c, 0, 0)),
+        out_shape=jax.ShapeDtypeStruct((2, 3, width // 2, dim), bf),
+        compiler_params=params(24),
+        cost_estimate=lasting(TIMES["outer"]),
+        name="outer",
+    )(g, normed)
+
+
 def exchange(x, axis, size, mask):
     return lax.ppermute(x, axis, [(i, i ^ mask) for i in range(size)])
 
 
-def reduce_over(x, axis, size):
-    masks = []
-    mask = 1
-    while mask < size:
-        masks.append(mask)
-        mask *= 2
-    me = lax.axis_index(axis)
-    for mask in masks:
-        half = x.shape[0] // 2
-        up = (me // mask) % 2
-        sent = lax.dynamic_slice_in_dim(x, (1 - up) * half, half, 0)
-        kept = lax.dynamic_slice_in_dim(x, up * half, half, 0)
-        got = exchange(sent, axis, size, mask)
-        x = (kept.astype(f32) + got.astype(f32)).astype(bf)
-    for mask in reversed(masks):
-        up = (me // mask) % 2
-        got = exchange(x, axis, size, mask)
-        first = jnp.where(up == 0, x, got)
-        second = jnp.where(up == 0, got, x)
-        x = jnp.concatenate([first, second], axis=0)
-    return x
+def tie(*values):
+    return lax.optimization_barrier(values)
 
 
 def add_bf(*parts):
@@ -493,11 +500,51 @@
     return total.astype(bf)
 
 
-def own_quarter(quarters, narrow):
-    one = exchange(quarters[1], "narrow", narrow, 1)
-    three = exchange(quarters[3], "narrow", narrow, 1)
-    peer = exchange(add_bf(quarters[2], three), "narrow", narrow, 2)
-    return add_bf(quarters[0], one, peer)
+def piece(x, index, count):
+    rows = x.shape[0] // count
+    return lax.dynamic_slice_in_dim(x, index * rows, rows, 0)
+
+
+class Wide:
+    def __init__(self, size):
+        self.size = size
+        self.me = lax.axis_index("wide")
+        self.groups = []
+        bit = 1
+        if size > 1:
+            self.groups.append((1, 2))
+            bit = 2
+        while bit < size:
+            members = min(4, size // bit)
+            self.groups.append((bit, members))
+            bit *= members
+
+    def at(self, group):
+        bit, members = group
+        return (self.me // bit) % members
+
+    def send(self, group, x):
+        bit, members = group
+        mine = self.at(group)
+        got = [
+            exchange(piece(x, mine ^ k, members), "wide", self.size, bit * k)
+            for k in range(1, members)
+        ]
+        return piece(x, mine, members), got
+
+    def gather(self, group, x):
+        bit, members = group
+        mine = self.at(group)
+        got = [exchange(x, "wide", self.size, bit * k) for k in range(1, members)]
+        if members == 2:
+            first = jnp.where(mine == 0, x, got[0])
+            second = jnp.where(mine == 0, got[0], x)
+            return jnp.concatenate([first, second], axis=0)
+        rows = x.shape[0]
+        out = jnp.zeros((members * rows,) + x.shape[1:], x.dtype)
+        for k, part in enumerate([x] + got):
+            out = lax.dynamic_update_slice_in_dim(out, part, (mine ^ k) * rows, 0)
+        return out
 
 
 def on_device(
@@ -530,101 +577,157 @@
     tokens3 = tokens.reshape(items, seq, dim)
     cot3 = cotangent.reshape(items, seq, dim)
     row = lambda x: x.reshape(1, dim)
+    mate = lambda x: exchange(x, "narrow", narrow, 1)
+    peer = lambda x: exchange(x, "narrow", narrow, 2)
+
+    ring = Wide(wide)
+    x_axis, tail_axes = ring.groups[0], ring.groups[1:]
+    across = lambda x: exchange(x, "wide", wide, 1)
+    low_half = (ring.me % 2).astype(jnp.int32)
+    half_dim = dim // 2
+
+    def my_half(x, axis):
+        return lax.dynamic_slice_in_dim(x, low_half * half_dim, half_dim, axis)
 
     w_flat = w_qkv.transpose(1, 2, 0)
-    small_in = jnp.concatenate(
-        [
-            jnp.pad(b_qv, ((0, 0), (0, dim - heads))),
-            jnp.pad(b_up.astype(f32), ((0, 5), (0, dim - units))),
-        ],
-        axis=0,
-    )
-
-    def others(x):
-        mate = exchange(x, "narrow", narrow, 1)
-        peer = exchange(x, "narrow", narrow, 2)
-        return x, mate, peer, exchange(peer, "narrow", narrow, 1)
-
-    qkv4 = others(w_flat)
-    out4 = others(w_out)
-    small4 = others(small_in)
-    up4 = others(w_up)
-    down4 = others(w_down)
-
-    def half(four, n, axis):
-        return jnp.concatenate([four[2 * n], four[2 * n + 1]], axis=axis)
-
-    w_half = [half(qkv4, n, 1) for n in range(2)]
-    out_half = [half(out4, n, 0) for n in range(2)]
-    b_half = [half([s[:2, :heads] for s in small4], n, 1) for n in range(2)]
-    up_bias = [half([s[2:3, :units] for s in small4], n, 1) for n in range(2)]
-
+    parts, rest = [], b_qv
+    for _ in range(3):
+        parts.append(lax.reduce_precision(rest, 8, 7))
+        rest = rest - parts[-1]
+    vectors = jnp.pad(jnp.concatenate(parts, axis=0).astype(bf), ((0, 0), (0, dim - heads)))
+    vectors = jnp.concatenate([vectors, b_up, jnp.zeros((1, dim), bf)], axis=0)
+    out_own = jnp.concatenate([w_out, vectors], axis=0)
+
+    def biases(block):
+        three = block[heads : heads + 6, :heads].astype(f32)
+        return three[0:2] + three[2:4] + three[4:6], block[heads + 6 : heads + 7, :units].astype(f32)
+
+    def halves(one, two):
+        b_one, u_one = biases(one)
+        b_two, u_two = biases(two)
+        return (
+            jnp.concatenate([one[:heads], two[:heads]], axis=0),
+            jnp.concatenate([b_one, b_two], axis=1),
+            jnp.concatenate([u_one, u_two], axis=1),
+        )
+
+    w_first = peer(my_half(w_flat, 2))
+    w_mate, out_mate = mate(w_flat), mate(out_own)
+    out_peer = peer(out_own)
+    up_mate, down_mate = mate(w_up), mate(w_down)
+    up_part, down_part = my_half(w_up, 0), my_half(w_down, 1)
+    gain1, bias1 = row(ln1_gain), row(ln1_bias)
+    w_a = jnp.concatenate([w_flat, w_mate], axis=1)
+    out_a, b_a, ub_a = halves(out_own, out_mate)
     q_a, k_a, v_a, mixed_a, log_a, normed1 = attend(
-        True, counts, tokens3, row(ln1_gain), row(ln1_bias), w_half[0], b_half[0], rows
-    )
-    q_b, k_b, v_b, mixed_b, log_b = attend(
-        False, counts, tokens3, row(ln1_gain), row(ln1_bias), w_half[1], b_half[1], rows
-    )
+        True, counts, tokens3, gain1, bias1, w_a, b_a, rows
+    )
+
+    log_a, w_first, out_peer, up_part = tie(log_a, w_first, out_peer, up_part)
+    w_second, up_first = across(w_first), peer(up_part)
+    out_far = mate(out_peer)
+    w_first, w_second, up_first, down_part = tie(w_first, w_second, up_first, down_part)
+    up_second, down_first = across(up_first), peer(down_part)
+    w_peer = jnp.where(
+        low_half == 0,
+        jnp.concatenate([w_first, w_second], axis=2),
+        jnp.concatenate([w_second, w_first], axis=2),
+    )
+    w_b = jnp.concatenate([w_peer, mate(w_peer)], axis=1)
+    out_b, b_b, ub_b = halves(out_peer, out_far)
+    q_b, k_b, v_b, mixed_b, log_b = attend(False, counts, tokens3, gain1, bias1, w_b, b_b, rows)
+
     middle, normed2, cot_pad = branch(
-        tokens3, cot3, mixed_a, mixed_b, out_half[0], out_half[1], row(b_out), row(ln2_gain), row(ln2_bias)
-    )
+        tokens3, cot3, mixed_a, mixed_b, out_a, out_b, row(b_out), row(ln2_gain), row(ln2_bias)
+    )
+    normed2, up_first, up_second, down_first = tie(normed2, up_first, up_second, down_first)
+    down_second = across(down_first)
+    ups = [up_first, up_second, mate(up_first), mate(up_second)]
+    flag = low_half.reshape(1)
     part, grad_part, dup_a, ddown_a, dbias_a = feed(
-        False, normed2, cot_pad, middle, None, row(b_down),
-        up4[0], up4[1], down4[0], down4[1], up_bias[0], seq,
-    )
+        False, flag, normed2, cot_pad, middle, None, row(b_down), [w_up, up_mate], [w_down, down_mate], ub_a, seq
+    )
+    part, down_first, down_second = tie(part, down_first, down_second)
+    downs = [down_first, down_second, mate(down_first), mate(down_second)]
+    got_up, got_down = mate(dup_a[1]), mate(ddown_a[1])
     layer_out, grad_norm2, dup_b, ddown_b, dbias_b = feed(
-        True, normed2, cot_pad, part, grad_part, row(b_down),
-        up4[2], up4[3], down4[2], down4[3], up_bias[1], seq,
-    )
+        True, flag, normed2, cot_pad, part, grad_part, row(b_down), ups, downs, ub_b, seq
+    )
+
+    grad_norm2, got_up, got_down = tie(grad_norm2, got_up, got_down)
+    far_up, far_down = mate(dup_b[1]), mate(ddown_b[1])
+    up_own = add_bf(dup_a[0], got_up)
+    down_keep, down_got = ring.send(x_axis, add_bf(ddown_a[0], got_down))
     grad_middle, gmix_a, gmix_b, dw_out, small_two = unbranch(
-        middle, cot_pad, grad_norm2, row(ln2_gain), mixed_a, mixed_b, out_half[0], out_half[1]
-    )
-    grad_one, dqkv_b, dbqv_b = unattend(counts, q_b, k_b, v_b, gmix_b, log_b, normed1, w_half[1])
-    input_grad, dqkv_a, dbqv_a, small_one = unattend(
-        counts, q_a, k_a, v_a, gmix_a, log_a, normed1, w_half[0],
-        (grad_one, grad_middle, tokens3, row(ln1_gain)),
-    )
-
-    feed_quarters = [
-        jnp.concatenate([du[n], dd[n]], axis=0)
-        for du, dd in ((dup_a, ddown_a), (dup_b, ddown_b))
-        for n in range(2)
-    ]
-    feed_sum = reduce_over(own_quarter(feed_quarters, narrow), "wide", wide)
-
-    vectors = [small_one[0:1], small_one[1:2]] + [small_two[n : n + 1] for n in range(4)]
-    quarters = []
-    for n in range(4):
-        dqkv, dbqv, dbias = ((dqkv_a, dbqv_a, dbias_a), (dqkv_b, dbqv_b, dbias_b))[n // 2]
+        middle, cot_pad, grad_norm2, row(ln2_gain), mixed_a, mixed_b, out_a, out_b
+    )
+    gmix_b, far_up, far_down = tie(gmix_b, far_up, far_down)
+    up_got = peer(add_bf(dup_b[0], far_up))
+    pair_keep, pair_got = ring.send(x_axis, add_bf(ddown_b[0], far_down))
+    grad_one, g_b, dbqv_b = unattend(counts, q_b, k_b, v_b, gmix_b, log_b, w_b)
+    g_b, pair_got, down_got = tie(g_b, pair_got[0], down_got[0])
+    pair_half = peer(add_bf(pair_keep, pair_got))
+    down_half = add_bf(down_keep, down_got)
+    dqkv_b = outer(g_b, normed1)
+
+    later = [jnp.zeros((2, dim), f32)] + [small_two[n : n + 1] for n in range(4)]
+
+    def block(n, dqkv, dbqv, dbias):
         at = n % 2
-        tail = vectors + [
+        tail = later + [
             dbias[:, at * units : (at + 1) * units],
             jnp.pad(dbqv[0:2, at * heads : (at + 1) * heads], ((0, 0), (0, dim - heads))),
         ]
         tail = jnp.concatenate(tail, axis=0)
-        total_rows = 4 * heads + tail.shape[0]
-        pad = -total_rows % (8 * wide)
+        pad = -(4 * heads + tail.shape[0]) % (8 * wide)
         tail = jnp.pad(tail, ((0, pad), (0, 0))).astype(bf)
-        quarters.append(
-            jnp.concatenate([dqkv[at].reshape(3 * heads, dim), dw_out[n], tail], axis=0)
-        )
-    rest_sum = reduce_over(own_quarter(quarters, narrow), "wide", wide).astype(f32)
-    feed_sum = feed_sum.astype(f32)
-    vec = rest_sum[4 * heads :]
+        return jnp.concatenate([dqkv[at].reshape(3 * heads, dim), dw_out[n], tail], axis=0)
+
+    far_rest = mate(block(3, dqkv_b, dbqv_b, dbias_b))
+    gmix_a, far_rest = tie(gmix_a, far_rest)
+    rest_keep, rest_got = ring.send(x_axis, add_bf(block(2, dqkv_b, dbqv_b, dbias_b), far_rest))
+    input_grad, g_a, dbqv_a, small_one = unattend(
+        counts, q_a, k_a, v_a, gmix_a, log_a, w_a, (grad_one, grad_middle, tokens3, gain1)
+    )
+    g_a, up_got, pair_half, rest_got = tie(g_a, up_got, pair_half, rest_got[0])
+    rest_half = peer(add_bf(rest_keep, rest_got))
+    dqkv_a = outer(g_a, normed1)
+    dqkv_a, firsts = tie(dqkv_a, small_one[0:2])
+    firsts = firsts + mate(firsts)
+    firsts = firsts + peer(firsts)
+    rest_mate = mate(block(1, dqkv_a, dbqv_a, dbias_a))
+
+    def over(groups, x):
+        for group in groups:
+            kept, got = ring.send(group, x)
+            x = add_bf(kept, *got)
+        return x
+
+    def back(groups, x):
+        for group in reversed(groups):
+            x = ring.gather(group, x)
+        return x
+
+    down_sum = back(ring.groups, over(tail_axes, add_bf(down_half, pair_half)))
+    up_sum = back(ring.groups, over(ring.groups, add_bf(up_own, up_got)))
+    rest_own = add_bf(block(0, dqkv_a, dbqv_a, dbias_a), rest_mate)
+    rest_own = lax.dynamic_update_slice_in_dim(rest_own, firsts.astype(bf), 4 * heads, 0)
+    rest_sum = back(ring.groups, over(tail_axes, add_bf(over([x_axis], rest_own), rest_half)))
+    vec = rest_sum[4 * heads :].astype(f32)
     return (
         layer_out.reshape(own_rows, dim),
         input_grad.reshape(own_rows, dim),
         vec[0],
         vec[1],
-        rest_sum[: 3 * heads].reshape(3, heads, dim).transpose(2, 0, 1),
+        rest_sum[: 3 * heads].astype(f32).reshape(3, heads, dim).transpose(2, 0, 1),
         vec[7:9, :heads],
-        rest_sum[3 * heads : 4 * heads],
+        rest_sum[3 * heads : 4 * heads].astype(f32),
         vec[4],
         vec[2],
         vec[3],
-        feed_sum[:dim],
+        up_sum.astype(f32),
         vec[6:7, :units],
-        feed_sum[dim:],
+        down_sum.astype(f32),
         vec[5],
     )
 

time: 415 us -> 326 us (0.79)
  waiting for transfers between devices: 196 us -> 96.3 us
  local copies, waits for them, and re-layouts: 33.9 us -> 42.3 us
    ppermute x33 -> x54, waiting for transfers between devices: 196 us -> 96.3 us  [exchange(): return lax.ppermute(x, axis, [(i, i ^ mask) for i in range(size)])]
    pallas_call x2 -> x4, Pallas kernels: 47.4 us -> 53.3 us  [the longest x2 47.7 us: feed(): pl.pallas_call(functools.partial(feed_kernel, last, per), grid_spec=pltpu...]
    dynamic_slice x6 -> x11, local copies, waits for them, and re-layouts: 1.87 us -> 6.87 us  [the longest x3 5.67 us: my_half(): return lax.dynamic_slice_in_dim(x, low_half * half_dim, half_dim, axis)]
    convert_element_type x4 -> x11, other arithmetic: 9.38 us -> 14.2 us  [add_bf(): return total.astype(bf)]
    unnamed x79 -> x132, local copies, waits for them, and re-layouts: 15.4 us -> 20.1 us
    pallas_call x2, Pallas kernels: 29.8 us -> 25.6 us  [unattend(): pl.pallas_call(functools.partial(unattend_kernel, final), grid_spec=pltpu...]
    concatenate x15 -> x14, other arithmetic: 9.84 us -> 6.35 us  [the longest x1 1.82 us: on_device(): out_own = jnp.concatenate([w_out, vectors], axis=0)]
    ppermute x33 -> x54, starting transfers between devices: 44.8 us -> 47.2 us  [exchange(): return lax.ppermute(x, axis, [(i, i ^ mask) for i in range(size)])]
  transfers between devices with their start and end apart: 33 -> 54, of which waited for: 16 -> 21; matrix products, arithmetic and copies ran while one was open for 11% -> 12% of each run, Pallas kernels for 26% -> 31%
where the time goes in v2:
time: 326 us; the launch traced here: 325 us
  Pallas kernels  108 us (33%)
  waiting for transfers between devices  96.3 us (30%)
  starting transfers between devices  47.2 us (14%)
  local copies, waits for them, and re-layouts  42.3 us (13%)
  other arithmetic  29.4 us (9%)
    ppermute x54, waiting for transfers between devices, exchange(): return lax.ppermute(x, axis, [(i, i ^ mask) for i in range(size)])  96.3 us
    pallas_call x2, Pallas kernels, feed(): pl.pallas_call(functools.partial(feed_kernel, last, per), grid_spec=pltpu...  47.7 us
    ppermute x54, starting transfers between devices, exchange(): return lax.ppermute(x, axis, [(i, i ^ mask) for i in range(size)])  47.2 us
    pallas_call x2, Pallas kernels, unattend(): pl.pallas_call(functools.partial(unattend_kernel, final), grid_spec=pltpu...  25.6 us
    pallas_call x2, Pallas kernels, attend(): pl.pallas_call(functools.partial(attend_kernel, first), grid_spec=pltpu.P...  20.2 us
    unnamed x132, local copies, waits for them, and re-layouts  20.1 us
    convert_element_type x11, other arithmetic, add_bf(): return total.astype(bf)  14.2 us
  transfers between devices with their start and end apart: 54, of which 21 were waited for; matrix products, arithmetic and copies ran while one was open for 12% of the time, Pallas kernels for 31%

profile of v2, /device:TPU:8, one launch (start us, length us, event | category | flops | bytes accessed | tf_op | source)
XLA Modules:
  0.0 324.6 jit_solution(15809559880992521442)
XLA Ops:
  12.6 10.1 %attend.2 = (bf16[3,288,384]{2,1,0:T(8,128)(2,1)S(1)}, bf16[3,288,384]{2,1,0:T(8,128)(2,1)S(1)}, bf16[3,288,384]{2,1,0:T(8,128)(2,1)S(1)}, bf16[3,288,384]{2,1,0...) custom-call(s32[3]{0:T(128)S(1)} %dynamic_slice.78.counts, ...), custom_call_target="tpu_custom_call" | custom-call | flops 11500000256 | tf_op jit(solution)/shard_map/attend/pallas_call | solution.py:128
  37.7 7.7 %collective-permute-done.4 = bf16[3,192,384]{2,1,0:T(8,128)(2,1)S(1)} collective-permute-done((bf16[3,192,384]{2,1,0:T(8,128)(2,1)}, bf16[3,192,384]{2,1,0:T(8,128)(2,1)S(1)}, u32[]{:S(2)}, u32[]{:S(2)}) %collective-permute-start.4) | collective-permute-done | bytes 442400 | tf_op jit(solution)/shard_map/ppermute | solution.py:489
  49.5 10.1 %attend.3 = (bf16[3,288,384]{2,1,0:T(8,128)(2,1)S(1)}, bf16[3,288,384]{2,1,0:T(8,128)(2,1)S(1)}, bf16[3,288,384]{2,1,0:T(8,128)(2,1)S(1)}, bf16[3,288,384]{2,1,0:T(8,128)(2,1)S(1)}, f32[3,8,288]{2,1,0:T(8,128)S(1)}) custom-call(s32[3]{0:T(128)S(1)} %dynamic_slice.78.counts, bf16[3,280,768]{2,1,0:T(8,128)(2,1)S(1)} %bitcast.47, ...), custom_call_target="tpu_custom_call" | custom-call | flops 11500000256 | tf_op jit(solution)/shard_map/attend/pallas_call | solution.py:128
  67.9 22.6 %feed.2 = (f32[3,288,768]{2,1,0:T(8,128)}, f32[3,288,768]{2,1,0:T(8,128)}, bf16[2,768,768]{2,1,0:T(8,128)(2,1)}, bf16[2,768,768]{2,1,0:T(8,128)(2,1)}, f32[1,1536]{1,0:T(1,128)}) custom-call(s32[1]{0:T(128)} %bitcast.low_half, bf16[3,288,768]{2,1,0:T(8,128)(2,1)} %copy-done.8, bf16[3,288,768]{2,1,0:T(8,128)(2,1)} %copy-done.6, f32[3,288,768]{2,1,0:T(8,128)} %copy-done.2, ...), custom_call_target="tpu_custom_call" | custom-call | flops 27599998976 | tf_op jit(solution)/shard_map/feed/pallas_call | solution.py:266
  95.8 25.1 %feed.3 = (f32[3,280,768]{2,1,0:T(8,128)}, f32[3,288,768]{2,1,0:T(8,128)}, bf16[2,768,768]{2,1,0:T(8,128)(2,1)}, bf16[2,768,768]{2,1,0:T(8,128)(2,1)}, f32[1,1536]{1,0:T(1,128)}) custom-call(s32[1]{0:T(128)} %bitcast.low_half, bf16[3,288,768]{2,1,0:T(8,128)(2,1)} %copy-done.8, bf16[3,288,768]{2,1,0:T(8,128)(2,1)} %copy-done.6, ...), custom_call_target="tpu_custom_call" | custom-call | flops 27599998976 | tf_op jit(solution)/shard_map/feed/pallas_call | solution.py:266
  128.7 5.8 %unbranch.1 = (f32[3,288,768]{2,1,0:T(8,128)S(1)}, bf16[3,288,384]{2,1,0:T(8,128)(2,1)S(1)}, bf16[3,288,384]{2,1,0:T(8,128)(2,1)S(1)}, bf16[4,192,768]{2,1,0:T(8,128)(2,1)S(1)}, f32[8,768]{1,0:T(8,128)S(1)}) custom-call(f32[3,288,768]{2,1,0:T(8,128)S(1)} %copy-done.3, bf16[3,288,768]{2,1,0:T(8,128)(2,1)S(1)} %copy-done.7, f32[3,288,768]{2,1,0:T(8,128)S(1)} %copy-done.19, ...), custom_call_target="tpu_custom_call" | custom-call | flops 6899999744 | tf_op jit(solution)/shard_map/unbranch/pallas_call | solution.py:345
  140.0 11.3 %unattend.2 = (f32[3,288,768]{2,1,0:T(8,128)S(1)}, bf16[3,288,1152]{2,1,0:T(8,128)(2,1)S(1)}, f32[8,384]{1,0:T(8,128)S(1)}) custom-call(s32[3]{0:T(128)S(1)} %dynamic_slice.78.counts, bf16[3,288,384]{2,1,0:T(8,128)(2,1)S(1)} %copy-done.31, bf16[3,288,384]{2,1,0:T(8,128)(2,1)S(1)} %copy-done.33, bf16[3,288,384]{2,1,0:T(8,128)(2,1)S(1)} %copy-done.35, ...), custom_call_target="tpu_custom_call" | custom-call | flops 14949999616 | tf_op jit(solution)/shard_map/unattend/pallas_call | solution.py:439
  151.5 4.6 %collective-permute-done.21 = bf16[384,768]{1,0:T(8,128)(2,1)S(1)} collective-permute-done((bf16[384,768]{1,0:T(8,128)(2,1)S(1)}, bf16[384,768]{1,0:T(8,128)(2,1)S(1)}, u32[]{:S(2)}, u32[]{:S(2)}) %collective-permute-start.21) | collective-permute-done | bytes 589856 | tf_op jit(solution)/shard_map/ppermute | solution.py:489
  156.1 2.8 outer.2
  161.1 3.1 fusion.5
  169.8 14.3 %unattend.3 = (f32[3,280,768]{2,1,0:T(8,128)}, bf16[3,288,1152]{2,1,0:T(8,128)(2,1)S(1)}, f32[8,384]{1,0:T(8,128)S(1)}, f32[8,768]{1,0:T(8,128)S(1)}) custom-call(s32[3]{0:T(128)S(1)} %dynamic_slice.78.counts, bf16[3,288,384]{2,1,0:T(8,128)(2,1)S(1)} %copy-done.25, bf16[3,288,384]{2,1,0:T(8,128)(2,1)S(1)} %copy-done.27, bf16[3,288,384]{2,1,0:T(8,128)(2,1)S(1)} %copy-done.29, ...), custom_call_target="tpu_custom_call" | custom-call | flops 14949999616 | tf_op jit(solution)/shard_map/unattend/pallas_call | solution.py:439
  190.4 15.2 %collective-permute-done.25 = bf16[384,768]{1,0:T(8,128)(2,1)} collective-permute-done((bf16[384,768]{1,0:T(8,128)(2,1)}, bf16[384,768]{1,0:T(8,128)(2,1)}, u32[]{:S(2)}, u32[]{:S(2)}) %collective-permute-start.25) | collective-permute-done | bytes 589856 | tf_op jit(solution)/shard_map/ppermute | solution.py:489
  222.1 4.5 %collective-permute-done.48 = bf16[96,768]{1,0:T(8,128)(2,1)S(1)} collective-permute-done((bf16[96,768]{1,0:T(8,128)(2,1)S(1)}, bf16[96,768]{1,0:T(8,128)(2,1)S(1)}, u32[]{:S(2)}, u32[]{:S(2)}) %collective-permute-start.48) | collective-permute-done | bytes 147488 | tf_op jit(solution)/shard_map/ppermute | solution.py:489
  233.0 4.3 %collective-permute-done.29 = f32[2,768]{1,0:T(2,128)S(1)} collective-permute-done((f32[2,768]{1,0:T(2,128)S(1)}, f32[2,768]{1,0:T(2,128)S(1)}, u32[]{:S(2)}, u32[]{:S(2)}) %collective-permute-start.29) | collective-permute-done | bytes 6176 | tf_op jit(solution)/shard_map/ppermute | solution.py:489
  245.1 3.0 collective-permute-start.52
  248.1 8.1 %collective-permute-done.41 = bf16[96,768]{1,0:T(8,128)(2,1)S(1)} collective-permute-done((bf16[96,768]{1,0:T(8,128)(2,1)S(1)}, bf16[96,768]{1,0:T(8,128)(2,1)S(1)}, u32[]{:S(2)}, u32[]{:S(2)}) %collective-permute-start.41) | collective-permute-done | bytes 147488 | tf_op jit(solution)/shard_map/ppermute | solution.py:489
  256.2 4.2 %collective-permute-done.42 = bf16[96,768]{1,0:T(8,128)(2,1)S(1)} collective-permute-done((bf16[96,768]{1,0:T(8,128)(2,1)S(1)}, bf16[96,768]{1,0:T(8,128)(2,1)S(1)}, u32[]{:S(2)}, u32[]{:S(2)}) %collective-permute-start.42) | collective-permute-done | bytes 147488 | tf_op jit(solution)/shard_map/ppermute | solution.py:489
  272.2 4.4 %collective-permute-done.33 = bf16[104,768]{1,0:T(8,128)(2,1)S(1)} collective-permute-done((bf16[104,768]{1,0:T(8,128)(2,1)S(1)}, bf16[104,768]{1,0:T(8,128)(2,1)S(1)}, u32[]{:S(2)}, u32[]{:S(2)}) %collective-permute-start.33) | collective-permute-done | bytes 159776 | tf_op jit(solution)/shard_map/ppermute | solution.py:489
  276.6 8.6 %collective-permute-done.34 = bf16[104,768]{1,0:T(8,128)(2,1)S(1)} collective-permute-done((bf16[104,768]{1,0:T(8,128)(2,1)S(1)}, bf16[104,768]{1,0:T(8,128)(2,1)S(1)}, u32[]{:S(2)}, u32[]{:S(2)}) %collective-permute-start.34) | collective-permute-done | bytes 159776 | tf_op jit(solution)/shard_map/ppermute | solution.py:489
  288.1 3.5 %collective-permute-start.36 = (bf16[104,768]{1,0:T(8,128)(2,1)S(1)}, bf16[104,768]{1,0:T(8,128)(2,1)S(1)}, u32[]{:S(2)}, u32[]{:S(2)}) collective-permute-start(bf16[104,768]{1,0:T(8,128)(2,1)S(1)} %get-tuple-element.161), channel_id=1, source_target_pairs={{0,16},{4,20},{8,24},{12,28},{16,0},{20,4},{24,8},{28,12},{1,17},{... | collective-permute-start | bytes 479240 | tf_op jit(solution)/shard_map/ppermute | solution.py:489
  291.6 5.2 %collective-permute-done.45 = bf16[96,768]{1,0:T(8,128)(2,1)S(1)} collective-permute-done((bf16[96,768]{1,0:T(8,128)(2,1)S(1)}, bf16[96,768]{1,0:T(8,128)(2,1)S(1)}, u32[]{:S(2)}, u32[]{:S(2)}) %collective-permute-start.45) | collective-permute-done | bytes 147488 | tf_op jit(solution)/shard_map/ppermute | solution.py:489
  299.5 3.1 collective-permute-done.37
  305.9 5.5 %collective-permute-done.46 = bf16[384,768]{1,0:T(8,128)(2,1)S(1)} collective-permute-done((bf16[384,768]{1,0:T(8,128)(2,1)S(1)}, bf16[384,768]{1,0:T(8,128)(2,1)S(1)}, u32[]{:S(2)}, u32[]{:S(2)}) %collective-permute-start.46) | collective-permute-done | bytes 589856 | tf_op jit(solution)/shard_map/ppermute | solution.py:489
  313.0 7.4 %collective-permute-done.38 = bf16[416,768]{1,0:T(8,128)(2,1)S(1)} collective-permute-done((bf16[416,768]{1,0:T(8,128)(2,1)S(1)}, bf16[416,768]{1,0:T(8,128)(2,1)S(1)}, u32[]{:S(2)}, u32[]{:S(2)}) %collective-permute-start.38) | collective-permute-done | bytes 639008 | tf_op jit(solution)/shard_map/ppermute | solution.py:489
  (331 shorter events, 128.4 us)
Async XLA Ops:
  3.4 23.9 %collective-permute-start.3 = (bf16[200,768]{1,0:T(8,128)(2,1)}, bf16[200,768]{1,0:T(8,128)(2,1)}, u32[]{:S(2)}, u32[]{:S(2)}) collective-permute-start(bf16[200,768]{1,0:T(8,128)(2,1)} %fusion.16), channel_id=1, source_target_pairs={{0,2},{1,3},{2,0},{3,1},{4,6},{5,7},{6,4},{7,5},{8,10},{9,11},{10,... | collective-permute-start | bytes 921608 | tf_op jit(solution)/shard_map/ppermute | solution.py:489
  6.7 20.5 %collective-permute-start.2 = (bf16[3,192,384]{2,1,0:T(8,128)(2,1)}, bf16[3,192,384]{2,1,0:T(8,128)(2,1)}, u32[]{:S(2)}, u32[]{:S(2)}) collective-permute-start(bf16[3,192,384]{2,1,0:T(8,128)(2,1)} %dynamic-slice_bitcast_fusion), channel_id=1, source_target_pairs={{0,2},{1,3},{2,0},{3,1},{4,6},{5,7},{6,4},{7,5},{8,10},{9,11},{10,... | collective-permute-start | bytes 1327112 | tf_op jit(solution)/shard_map/ppermute | solution.py:489
  7.2 60.7 %collective-permute-start.10 = (bf16[768,768]{1,0:T(8,128)(2,1)}, bf16[768,768]{1,0:T(8,128)(2,1)}, u32[]{:S(2)}, u32[]{:S(2)}) collective-permute-start(bf16[768,768]{1,0:T(8,128)(2,1)} %refs_0_.1), channel_id=1, source_target_pairs={{0,1},{1,0},{2,3},{3,2},{4,5},{5,4},{6,7},{7,6},{8,9},{9,8},{10,11... | collective-permute-start | bytes 3538952 | tf_op jit(solution)/shard_map/ppermute | solution.py:489
  9.8 58.1 %collective-permute-start.11 = (bf16[768,768]{1,0:T(8,128)(2,1)}, bf16[768,768]{1,0:T(8,128)(2,1)}, u32[]{:S(2)}, u32[]{:S(2)}) collective-permute-start(bf16[768,768]{1,0:T(8,128)(2,1)} %refs_2_.1), channel_id=1, source_target_pairs={{0,1},{1,0},{2,3},{3,2},{4,5},{5,4},{6,7},{7,6},{8,9},{9,8},{10,11... | collective-permute-start | bytes 3538952 | tf_op jit(solution)/shard_map/ppermute | solution.py:489
  27.2 18.1 %collective-permute-start.5 = (bf16[384,768]{1,0:T(8,128)(2,1)}, bf16[384,768]{1,0:T(8,128)(2,1)}, u32[]{:S(2)}, u32[]{:S(2)}) collective-permute-start(bf16[384,768]{1,0:T(8,128)(2,1)} %constant_dynamic-slice_fusion.15), channel_id=1, source_target_pairs={{0,2},{1,3},{2,0},{3,1},{4,6},{5,7},{6,4},{7,5},{8,10},{9,11},{10,... | collective-permute-start | bytes 1769480 | tf_op jit(solution)/shard_map/ppermute | solution.py:489
  47.1 18.8 %collective-permute-start.8 = (bf16[384,768]{1,0:T(8,128)(2,1)}, bf16[384,768]{1,0:T(8,128)(2,1)}, u32[]{:S(2)}, u32[]{:S(2)}) collective-permute-start(bf16[384,768]{1,0:T(8,128)(2,1)} %collective-permute-done.5.refs_0_), channel_id=1, source_target_pairs={{0,4},{4,0},{8,12},{12,8},{16,20},{20,16},{24,28},{28,24},{1,5},{5... | collective-permute-start | bytes 1769480 | tf_op jit(solution)/shard_map/ppermute | solution.py:489
  65.9 24.6 %collective-permute-start.12 = (bf16[768,384]{1,0:T(8,128)(2,1)}, bf16[768,384]{1,0:T(8,128)(2,1)}, u32[]{:S(2)}, u32[]{:S(2)}) collective-permute-start(bf16[768,384]{1,0:T(8,128)(2,1)} %collective-permute-done.9.refs_4_), channel_id=1, source_target_pairs={{0,4},{4,0},{8,12},{12,8},{16,20},{20,16},{24,28},{28,24},{1,5},{5... | collective-permute-start | bytes 1769480 | tf_op jit(solution)/shard_map/ppermute | solution.py:489
  67.4 27.9 %collective-permute-start.13 = (bf16[384,768]{1,0:T(8,128)(2,1)}, bf16[384,768]{1,0:T(8,128)(2,1)}, u32[]{:S(2)}, u32[]{:S(2)}) collective-permute-start(bf16[384,768]{1,0:T(8,128)(2,1)} %collective-permute-done.5.refs_0_), channel_id=1, source_target_pairs={{0,1},{1,0},{2,3},{3,2},{4,5},{5,4},{6,7},{7,6},{8,9},{9,8},{10,11... | collective-permute-start | bytes 1769480 | tf_op jit(solution)/shard_map/ppermute | solution.py:489
  67.4 28.3 %collective-permute-start.14 = (bf16[384,768]{1,0:T(8,128)(2,1)}, bf16[384,768]{1,0:T(8,128)(2,1)}, u32[]{:S(2)}, u32[]{:S(2)}) collective-permute-start(bf16[384,768]{1,0:T(8,128)(2,1)} %collective-permute-done.8.refs_1_), channel_id=1, source_target_pairs={{0,1},{1,0},{2,3},{3,2},{4,5},{5,4},{6,7},{7,6},{8,9},{9,8},{10,11... | collective-permute-start | bytes 1769480 | tf_op jit(solution)/shard_map/ppermute | solution.py:489
  94.1 26.8 %collective-permute-start.17 = (bf16[768,768]{1,0:T(8,128)(2,1)}, bf16[768,768]{1,0:T(8,128)(2,1)}, u32[]{:S(2)}, u32[]{:S(2)}) collective-permute-start(bf16[768,768]{1,0:T(8,128)(2,1)} %slice_bitcast_fusion.3), channel_id=1, source_target_pairs={{0,1},{1,0},{2,3},{3,2},{4,5},{5,4},{6,7},{7,6},{8,9},{9,8},{10,11... | collective-permute-start | bytes 3538952 | tf_op jit(solution)/shard_map/ppermute | solution.py:489
  95.3 25.6 %collective-permute-start.18 = (bf16[768,768]{1,0:T(8,128)(2,1)}, bf16[768,768]{1,0:T(8,128)(2,1)S(1)}, u32[]{:S(2)}, u32[]{:S(2)}) collective-permute-start(bf16[768,768]{1,0:T(8,128)(2,1)} %slice_bitcast_fusion.2), channel_id=1, source_target_pairs={{0,1},{1,0},{2,3},{3,2},{4,5},{5,4},{6,7},{7,6},{8,9},{9,8},{10,11... | collective-permute-start | bytes 3538952 | tf_op jit(solution)/shard_map/ppermute | solution.py:489
  128.0 23.5 %collective-permute-start.22 = (bf16[384,768]{1,0:T(8,128)(2,1)S(1)}, bf16[384,768]{1,0:T(8,128)(2,1)S(1)}, u32[]{:S(2)}, u32[]{:S(2)}) collective-permute-start(bf16[384,768]{1,0:T(8,128)(2,1)S(1)} %constant_dynamic-slice_fusion.12), channel_id=1, source_target_pairs={{0,4},{4,0},{8,12},{12,8},{16,20},{20,16},{24,28},{28,24},{1,5},{5... | collective-permute-start | bytes 1769480 | tf_op jit(solution)/shard_map/ppermute | solution.py:489
  164.2 41.3 %collective-permute-start.24 = (bf16[768,768]{1,0:T(8,128)(2,1)}, bf16[768,768]{1,0:T(8,128)(2,1)}, u32[]{:S(2)}, u32[]{:S(2)}) collective-permute-start(bf16[768,768]{1,0:T(8,128)(2,1)} %fusion.5), channel_id=1, source_target_pairs={{0,2},{1,3},{2,0},{3,1},{4,6},{5,7},{6,4},{7,5},{8,10},{9,11},{10,... | collective-permute-start | bytes 3538952 | tf_op jit(solution)/shard_map/ppermute | solution.py:489
  187.4 18.1 %collective-permute-start.26 = (bf16[416,768]{1,0:T(8,128)(2,1)}, bf16[416,768]{1,0:T(8,128)(2,1)}, u32[]{:S(2)}, u32[]{:S(2)}) collective-permute-start(bf16[416,768]{1,0:T(8,128)(2,1)} %constant_dynamic-slice_fusion.11), channel_id=1, source_target_pairs={{0,4},{4,0},{8,12},{12,8},{16,20},{20,16},{24,28},{28,24},{1,5},{5... | collective-permute-start | bytes 1916936 | tf_op jit(solution)/shard_map/ppermute | solution.py:489
  211.0 18.9 %collective-permute-start.27 = (bf16[832,768]{1,0:T(8,128)(2,1)S(1)}, bf16[832,768]{1,0:T(8,128)(2,1)S(1)}, u32[]{:S(2)}, u32[]{:S(2)}) collective-permute-start(bf16[832,768]{1,0:T(8,128)(2,1)S(1)} %fusion.11), channel_id=1, source_target_pairs={{0,1},{1,0},{2,3},{3,2},{4,5},{5,4},{6,7},{7,6},{8,9},{9,8},{10,11... | collective-permute-start | bytes 3833864 | tf_op jit(solution)/shard_map/ppermute | solution.py:489
  220.0 19.0 %collective-permute-start.39 = (bf16[384,768]{1,0:T(8,128)(2,1)S(1)}, bf16[384,768]{1,0:T(8,128)(2,1)S(1)}, u32[]{:S(2)}, u32[]{:S(2)}) collective-permute-start(bf16[384,768]{1,0:T(8,128)(2,1)S(1)} %constant_dynamic-slice_fusion.6), channel_id=1, source_target_pairs={{0,4},{4,0},{8,12},{12,8},{16,20},{20,16},{24,28},{28,24},{1,5},{5... | collective-permute-start | bytes 1769480 | tf_op jit(solution)/shard_map/ppermute | solution.py:489
  220.6 40.0 %collective-permute-start.31 = (bf16[416,768]{1,0:T(8,128)(2,1)S(1)}, bf16[416,768]{1,0:T(8,128)(2,1)S(1)}, u32[]{:S(2)}, u32[]{:S(2)}) collective-permute-start(bf16[416,768]{1,0:T(8,128)(2,1)S(1)} %add_convert_fusion.4), channel_id=1, source_target_pairs={{0,2},{1,3},{2,0},{3,1},{4,6},{5,7},{6,4},{7,5},{8,10},{9,11},{10,... | collective-permute-start | bytes 1916936 | tf_op jit(solution)/shard_map/ppermute | solution.py:489
  237.4 23.2 %collective-permute-start.30 = (bf16[416,768]{1,0:T(8,128)(2,1)S(1)}, bf16[416,768]{1,0:T(8,128)(2,1)S(1)}, u32[]{:S(2)}, u32[]{:S(2)}) collective-permute-start(bf16[416,768]{1,0:T(8,128)(2,1)S(1)} %constant_dynamic-slice_fusion.10), channel_id=1, source_target_pairs={{0,4},{4,0},{8,12},{12,8},{16,20},{20,16},{24,28},{28,24},{1,5},{5... | collective-permute-start | bytes 1916936 | tf_op jit(solution)/shard_map/ppermute | solution.py:489
  245.1 19.4 %collective-permute-start.52 = (bf16[96,768]{1,0:T(8,128)(2,1)S(1)}, bf16[96,768]{1,0:T(8,128)(2,1)S(1)}, u32[]{:S(2)}, u32[]{:S(2)}) collective-permute-start(bf16[96,768]{1,0:T(8,128)(2,1)S(1)} %get-tuple-element.157), channel_id=1, source_target_pairs={{0,24},{4,28},{8,16},{12,20},{16,8},{20,12},{24,0},{28,4},{1,25},{... | collective-permute-start | bytes 442376 | tf_op jit(solution)/shard_map/ppermute | solution.py:489
  263.9 21.3 %collective-permute-start.34 = (bf16[104,768]{1,0:T(8,128)(2,1)S(1)}, bf16[104,768]{1,0:T(8,128)(2,1)S(1)}, u32[]{:S(2)}, u32[]{:S(2)}) collective-permute-start(bf16[104,768]{1,0:T(8,128)(2,1)S(1)} %get-tuple-element.177), channel_id=1, source_target_pairs={{0,24},{4,28},{8,16},{12,20},{16,8},{20,12},{24,0},{28,4},{1,25},{... | collective-permute-start | bytes 479240 | tf_op jit(solution)/shard_map/ppermute | solution.py:489
  264.6 39.6 %collective-permute-start.53 = (bf16[384,768]{1,0:T(8,128)(2,1)S(1)}, bf16[384,768]{1,0:T(8,128)(2,1)S(1)}, u32[]{:S(2)}, u32[]{:S(2)}) collective-permute-start(bf16[384,768]{1,0:T(8,128)(2,1)S(1)} %constant_dynamic-update-slice_fusion), channel_id=1, source_target_pairs={{0,4},{4,0},{8,12},{12,8},{16,20},{20,16},{24,28},{28,24},{1,5},{5... | collective-permute-start | bytes 1769480 | tf_op jit(solution)/shard_map/ppermute | solution.py:489
  267.4 20.7 %collective-permute-start.44 = (bf16[96,768]{1,0:T(8,128)(2,1)S(1)}, bf16[96,768]{1,0:T(8,128)(2,1)S(1)}, u32[]{:S(2)}, u32[]{:S(2)}) collective-permute-start(bf16[96,768]{1,0:T(8,128)(2,1)S(1)} %get-tuple-element.159), channel_id=1, source_target_pairs={{0,16},{4,20},{8,24},{12,28},{16,0},{20,4},{24,8},{28,12},{1,17},{... | collective-permute-start | bytes 442376 | tf_op jit(solution)/shard_map/ppermute | solution.py:489
  270.8 25.9 %collective-permute-start.45 = (bf16[96,768]{1,0:T(8,128)(2,1)S(1)}, bf16[96,768]{1,0:T(8,128)(2,1)S(1)}, u32[]{:S(2)}, u32[]{:S(2)}) collective-permute-start(bf16[96,768]{1,0:T(8,128)(2,1)S(1)} %get-tuple-element.159), channel_id=1, source_target_pairs={{0,24},{4,28},{8,16},{12,20},{16,8},{20,12},{24,0},{28,4},{1,25},{... | collective-permute-start | bytes 442376 | tf_op jit(solution)/shard_map/ppermute | solution.py:489
  302.6 17.8 %collective-permute-start.38 = (bf16[416,768]{1,0:T(8,128)(2,1)S(1)}, bf16[416,768]{1,0:T(8,128)(2,1)S(1)}, u32[]{:S(2)}, u32[]{:S(2)}) collective-permute-start(bf16[416,768]{1,0:T(8,128)(2,1)S(1)} %constant_dynamic-update-slice_fusion.8), channel_id=1, source_target_pairs={{0,4},{4,0},{8,12},{12,8},{16,20},{20,16},{24,28},{28,24},{1,5},{5... | collective-permute-start | bytes 1916936 | tf_op jit(solution)/shard_map/ppermute | solution.py:489
  (96 other events, 635.6 us)
